TPU v7x, 32 devices: a whole 2x2x4 slice. The times are simulated.
32 devices in a mesh: rep: 8 (over y, x, core), grp: 4 (over z).
Axes of the slice: x: 2, y: 2, z: 4, core: 2. Of those that a mesh axis runs over, the one named last changes fastest.
Arguments:
- latents: bfloat16 [8, 1024, 1152], P('rep', 'grp'), may hold values from -6 to 6
- condition: bfloat16 [8, 1152], P('rep'), may hold values from -6 to 6
- cotangent: bfloat16 [8, 1024, 1152], P('rep', 'grp'), may hold values from -6 to 6
- ada_weight: bfloat16 [1152, 6912], P('grp'), may hold values from -0.1875 to 0.1875
- ada_bias: bfloat16 [6912], P('grp'), may hold values from -3 to 3
- qkv_weight: bfloat16 [1152, 3456], P('grp'), may hold values from -0.1875 to 0.1875
- qv_bias: bfloat16 [2304], P('grp'), may hold values from -3 to 3
- proj_weight: bfloat16 [1152, 1152], P('grp'), may hold values from -6 to 6
- proj_bias: bfloat16 [1152], P('grp'), may hold values from -3 to 3
- fc1_weight: bfloat16 [1152, 4608], P('grp'), may hold values from -0.1875 to 0.1875
- fc1_bias: bfloat16 [4608], P('grp'), may hold values from -3 to 3
- fc2_weight: bfloat16 [4608, 1152], P('grp'), may hold values from -0.09375 to 0.09375
- fc2_bias: bfloat16 [1152], P('grp'), may hold values from -3 to 3
Outputs:
- output: float32 [8, 1024, 1152], P('rep', 'grp')
- grad_latents: float32 [8, 1024, 1152], P('rep', 'grp')
- grad_condition: float32 [8, 1152], P('rep')
- grad_ada_weight: float32 [1152, 6912], P('grp')
- grad_ada_bias: float32 [6912], P('grp')
- grad_qkv_weight: float32 [1152, 3456], P('grp')
- grad_qv_bias: float32 [2304], P('grp')
- grad_proj_weight: float32 [1152, 1152], P('grp')
- grad_proj_bias: float32 [1152], P('grp')
- grad_fc1_weight: float32 [1152, 4608], P('grp')
- grad_fc1_bias: float32 [4608], P('grp')
- grad_fc2_weight: float32 [4608, 1152], P('grp')
- grad_fc2_bias: float32 [1152], P('grp')
All inputs are finite; a program needn't handle non-finite values.
Results may differ from a plain program's by a relative error of at most 0.019.
Values may be sent and summed in bfloat16 or wider, within the bound.
No kernel may reach another device: no remote copies, remote signals or barrier semaphores. Data moves between devices by JAX's collectives and lax.ppermute only.
A program may use at most 320 MiB of HBM per device.

v0:
```python
import functools
import math

import jax
import jax.numpy as jnp
from jax import lax
from jax.experimental import pallas as pl
from jax.experimental.pallas import tpu as pltpu
from jax.sharding import PartitionSpec as P


HDIM = 72
EPS = 1e-06
LOG2E = math.log2(math.e)
BF = jnp.bfloat16
F32 = jnp.float32
NT = (((1,), (1,)), ((), ()))
NN = (((1,), (0,)), ((), ()))
TN = (((0,), (0,)), ((), ()))


def dot(a, b, dims=NN):
    return lax.dot_general(a, b, dims, preferred_element_type=F32)


def parts_of(ref, rows, h):
    width = ref.shape[1] // 3
    return [ref[rows, k * width + h * HDIM : k * width + (h + 1) * HDIM] for k in range(3)]


def attend_kernel(heads, tile, x_ref, o_ref, lse_ref):
    factor = HDIM**-0.5 * LOG2E
    rows = pl.ds(pl.multiple_of(pl.program_id(0) * tile, tile), tile)
    for h in range(heads):
        queries = parts_of(x_ref, rows, h)[0]
        _, keys, values = parts_of(x_ref, slice(None), h)
        scores = dot(keys, queries, NT)
        top = jnp.max(scores, axis=0, keepdims=True)
        weights = jnp.exp2((scores - top) * factor)
        total = jnp.sum(weights, axis=0, keepdims=True)
        mixed = dot(values, weights.astype(BF), TN)
        o_ref[:, h * HDIM : (h + 1) * HDIM] = (mixed / total).T.astype(BF)
        lse_ref[h : h + 1, :] = top * factor + jnp.log2(total)


def attend(x, tile):
    seq, width = x.shape[0], x.shape[1] // 3
    heads = width // HDIM
    return pl.pallas_call(
        functools.partial(attend_kernel, heads, tile),
        grid=(seq // tile,),
        in_specs=[pl.BlockSpec((seq, 3 * width), lambda i: (0, 0))],
        out_specs=[
            pl.BlockSpec((tile, width), lambda i: (i, 0)),
            pl.BlockSpec((heads, tile), lambda i: (0, i)),
        ],
        out_shape=[
            jax.ShapeDtypeStruct((seq, width), BF),
            jax.ShapeDtypeStruct((heads, seq), F32),
        ],
        cost_estimate=pl.CostEstimate(
            flops=4 * seq * seq * width,
            bytes_accessed=8 * seq * width,
            transcendentals=heads * seq * seq,
        ),
        name="attend",
    )(x)


def attend_back_kernel(heads, tile, x_ref, g_ref, lse_ref, d_ref, sum_ref, dk_acc, dv_acc):
    step = pl.program_id(0)
    scale = HDIM**-0.5
    width = heads * HDIM
    rows = pl.ds(pl.multiple_of(step * tile, tile), tile)

    @pl.when(step == 0)
    def _():
        dk_acc[...] = jnp.zeros_like(dk_acc)
        dv_acc[...] = jnp.zeros_like(dv_acc)
        sum_ref[...] = jnp.zeros_like(sum_ref)

    for h in range(heads):
        cols = slice(h * HDIM, (h + 1) * HDIM)
        queries = parts_of(x_ref, rows, h)[0]
        _, keys, values = parts_of(x_ref, slice(None), h)
        grads = g_ref[:, cols]
        probs = jnp.exp2(dot(keys, queries, NT) * (scale * LOG2E) - lse_ref[h : h + 1, :])
        dprobs = dot(values, grads, NT)
        delta = jnp.sum(probs * dprobs, axis=0, keepdims=True)
        dscores = (probs * (dprobs - delta)).astype(BF)
        dq = (dot(keys, dscores, TN) * scale).T
        d_ref[rows, cols] = dq.astype(BF)
        sum_ref[0:1, cols] += jnp.sum(dq, axis=0, keepdims=True)
        dk_acc[h] += dot(dscores, queries)
        dv_acc[h] += dot(probs.astype(BF), grads)

    @pl.when(step == pl.num_programs(0) - 1)
    def _():
        for h in range(heads):
            start = width + h * HDIM
            d_ref[:, start : start + HDIM] = (dk_acc[h] * scale).astype(BF)
            d_ref[:, width + start : width + start + HDIM] = dv_acc[h].astype(BF)
            sum_ref[1:2, h * HDIM : (h + 1) * HDIM] = jnp.sum(dv_acc[h], axis=0, keepdims=True)


def attend_back(x, grads, lse, tile):
    seq, width = x.shape[0], x.shape[1] // 3
    heads = width // HDIM
    whole = pl.BlockSpec((seq, 3 * width), lambda i: (0, 0))
    return pl.pallas_call(
        functools.partial(attend_back_kernel, heads, tile),
        grid=(seq // tile,),
        in_specs=[
            whole,
            pl.BlockSpec((tile, width), lambda i: (i, 0)),
            pl.BlockSpec((heads, tile), lambda i: (0, i)),
        ],
        out_specs=[whole, pl.BlockSpec((8, width), lambda i: (0, 0))],
        out_shape=[
            jax.ShapeDtypeStruct((seq, 3 * width), BF),
            jax.ShapeDtypeStruct((8, width), F32),
        ],
        scratch_shapes=[pltpu.VMEM((heads, seq, HDIM), F32), pltpu.VMEM((heads, seq, HDIM), F32)],
        cost_estimate=pl.CostEstimate(
            flops=10 * seq * seq * width,
            bytes_accessed=14 * seq * width,
            transcendentals=heads * seq * seq,
        ),
        name="attend_back",
    )(x, grads, lse)


def place_kernel(counts, cuts, table_ref, *refs):
    pieces, outs = refs[: len(counts)], refs[len(counts) :]
    start = 0
    for piece, count in zip(pieces, counts):

        def put(i, carry, piece=piece, start=start):
            for k, ((low, high), out) in enumerate(zip(cuts, outs)):
                cols = piece.shape[2]
                value = piece[i, low:high, :].astype(out.dtype)
                row = table_ref[2 * k, start + i]
                if out.shape[2] == cols:
                    out[row] = value
                else:
                    out[row, :, pl.ds(pl.multiple_of(table_ref[2 * k + 1, start + i] * cols, 128), cols)] = value
            return carry

        lax.fori_loop(0, count, put, 0)
        start += count


def place(pieces, places, outs, cuts=None):
    counts = [piece.shape[0] for piece in pieces]
    places = [p if isinstance(p, tuple) else (p, jnp.zeros_like(p)) for p in places]
    cuts = cuts or [(0, pieces[0].shape[1])]
    whole = pl.BlockSpec(memory_space=pltpu.VMEM)
    size = sum(2 * math.prod(x.shape) for x in pieces)
    return pl.pallas_call(
        functools.partial(place_kernel, counts, cuts),
        in_specs=[pl.BlockSpec(memory_space=pltpu.SMEM)] + [whole] * len(pieces),
        out_specs=[whole] * len(outs),
        out_shape=outs,
        cost_estimate=pl.CostEstimate(flops=0, bytes_accessed=3 * size, transcendentals=0),
        name="place",
    )(jnp.stack([x for p in places for x in p]).astype(jnp.int32), *pieces)


def last_kernel(pair, width, place_ref, x_ref, proj_ref, qkv_ref):
    grp = place_ref[0]
    rows = width // pair // 2
    start = width // 2
    for core in range(2):
        proj_ref[0, :, core * start : (core + 1) * start] = x_ref[0, core, :, :start].astype(F32)
    for block in range(2 * pair):
        index = lax.rem(grp - block // 2 + pair * 2, pair)
        for at, sender in [(a, c) for a in range(pair) for c in range(2)]:
            first = start + (at % (pair // 2) * 2 + (block % 2 ^ sender)) * 3 * rows

            @pl.when((index == at) & (grp // pair == sender))
            def _():
                for kind in range(3):
                    qkv_ref[0, :, kind * width + block * rows : kind * width + (block + 1) * rows] = x_ref[
                        0, at // (pair // 2), :, first + kind * rows : first + (kind + 1) * rows
                    ].astype(F32)


def place_last(x, grp, pair, width):
    chips, _, share, cols = x.shape
    return pl.pallas_call(
        functools.partial(last_kernel, pair, width),
        grid_spec=pltpu.PrefetchScalarGridSpec(
            num_scalar_prefetch=1,
            grid=(chips,),
            in_specs=[pl.BlockSpec((1, 2, share, cols), lambda i, table: (i, 0, 0, 0))],
            out_specs=[
                pl.BlockSpec((1, share, width), lambda i, table: (i, 0, 0)),
                pl.BlockSpec((1, share, 3 * width), lambda i, table: (i, 0, 0)),
            ],
        ),
        out_shape=[
            jax.ShapeDtypeStruct((chips, share, width), F32),
            jax.ShapeDtypeStruct((chips, share, 3 * width), F32),
        ],
        cost_estimate=pl.CostEstimate(
            flops=0, bytes_accessed=24 * chips * share * width, transcendentals=0
        ),
        name="place_last",
    )(jnp.stack([grp]).astype(jnp.int32), x)


def take_columns_kernel(grps, place_ref, x_ref, out_ref):
    cols = out_ref.shape[1] // grps
    for rank in range(4):

        @pl.when(place_ref[0] == rank)
        def _():
            for block in range(grps):
                start = (4 * block + rank) * cols
                out_ref[:, block * cols : (block + 1) * cols] = x_ref[0, :, start : start + cols]


def take_columns(x, rank, line, grps):
    _, share, cols = x.shape
    return pl.pallas_call(
        functools.partial(take_columns_kernel, grps),
        grid_spec=pltpu.PrefetchScalarGridSpec(
            num_scalar_prefetch=1,
            grid=(1,),
            in_specs=[pl.BlockSpec((1, share, cols), lambda i, table: (table[1], 0, 0))],
            out_specs=pl.BlockSpec((share, cols // 4), lambda i, table: (0, 0)),
        ),
        out_shape=jax.ShapeDtypeStruct((share, cols // 4), BF),
        cost_estimate=pl.CostEstimate(flops=0, bytes_accessed=3 * share * cols, transcendentals=0),
        name="take_columns",
    )(jnp.stack([rank, line]).astype(jnp.int32), x)


def fc_kernel(fc1_rows, grps, x_ref, fc1_ref, fc2_ref):
    cols = x_ref.shape[3] // grps
    for rank in range(4):
        for block in range(grps):
            start = (4 * block + rank) * cols
            fc1_ref[0, :, start : start + cols] = x_ref[
                0, rank, :fc1_rows, block * cols : (block + 1) * cols
            ].astype(F32)
        fc2_ref[rank, 0] = x_ref[0, rank, fc1_rows:, :].astype(F32)


def place_fc(x, fc1_rows, grps):
    lines, _, both, cols = x.shape
    fc2_rows = both - fc1_rows
    return pl.pallas_call(
        functools.partial(fc_kernel, fc1_rows, grps),
        grid=(lines,),
        in_specs=[pl.BlockSpec((1, 4, both, cols), lambda i: (i, 0, 0, 0))],
        out_specs=[
            pl.BlockSpec((1, fc1_rows, 4 * cols), lambda i: (i, 0, 0)),
            pl.BlockSpec((4, 1, fc2_rows, cols), lambda i: (0, i, 0, 0)),
        ],
        out_shape=[
            jax.ShapeDtypeStruct((lines, fc1_rows, 4 * cols), F32),
            jax.ShapeDtypeStruct((4, lines, fc2_rows, cols), F32),
        ],
        cost_estimate=pl.CostEstimate(
            flops=0, bytes_accessed=24 * lines * both * cols, transcendentals=0
        ),
        name="place_fc",
    )(x)


def take_heads_kernel(pair, place_ref, x_ref, out_ref):
    grp = place_ref[1]
    width = x_ref.shape[2] // 3
    rows = width // pair // 2
    for unit in range(pair):
        index = lax.rem(grp - unit + pair * 2, pair)
        for core in range(2):
            for kind in range(3):
                start = kind * width + (2 * unit + core) * rows
                out_ref[index, core, :, kind * rows : (kind + 1) * rows] = x_ref[0, :, start : start + rows]


def heads_for(x, core, grp, chip):
    _, share, cols = x.shape
    grps = lax.axis_size("grp")
    rows = cols // 3 // grps
    return pl.pallas_call(
        functools.partial(take_heads_kernel, grps // 2),
        grid_spec=pltpu.PrefetchScalarGridSpec(
            num_scalar_prefetch=1,
            grid=(1,),
            in_specs=[pl.BlockSpec((1, share, cols), lambda i, table: (table[2], 0, 0))],
            out_specs=pl.BlockSpec((grps // 2, 2, share, 3 * rows), lambda i, table: (0, 0, 0, 0)),
        ),
        out_shape=jax.ShapeDtypeStruct((grps // 2, 2, share, 3 * rows), BF),
        cost_estimate=pl.CostEstimate(flops=0, bytes_accessed=4 * share * cols, transcendentals=0),
        name="take_heads",
    )(jnp.stack([core, grp, chip]).astype(jnp.int32), x)


def layer_norm(values):
    centre = values - jnp.mean(values, axis=-1, keepdims=True)
    inverse = lax.rsqrt(jnp.mean(centre * centre, axis=-1, keepdims=True) + EPS)
    return (centre * inverse, inverse)


def norm_back(normed, inverse, grad):
    return inverse * (
        grad
        - jnp.mean(grad, axis=-1, keepdims=True)
        - normed * jnp.mean(grad * normed, axis=-1, keepdims=True)
    )


def silu_float(values):
    return values * jax.nn.sigmoid(values)


def gelu_float(values):
    return jax.nn.gelu(values, approximate=True)


def block_step(
    reps,
    grps,
    latents,
    condition,
    cotangent,
    ada_weight,
    ada_bias,
    qkv_weight,
    qv_bias,
    proj_weight,
    proj_bias,
    fc1_weight,
    fc1_bias,
    fc2_weight,
    fc2_bias,
):
    width = latents.shape[2]
    part = latents.shape[1]
    seq = part * grps
    rows = width // grps
    hidden_width = fc1_weight.shape[1]
    chips = reps // 2
    pair = grps // 2
    share = rows // chips
    rep, grp = lax.axis_index("rep"), lax.axis_index("grp")
    chip, core = rep // 2, rep % 2
    quarter = hidden_width // 4
    mesh_axes = ("rep", "grp")
    tile = min(256, seq)
    served = grp // pair
    block = grp % pair * 2 + core
    lines = reps // 4
    line, rank = rep // 4, rep % 4
    fc1_rows, fc2_rows = rows // lines, quarter // grps // lines
    same_rank = [[g * reps + r for g in range(grps) for r in range(f, reps, 4)] for f in range(4)]

    def shift(x, amount):
        return lax.ppermute(x, "grp", [(g, (g + amount) % grps) for g in range(grps)])

    def partner(x):
        return lax.ppermute(x, "rep", [(r, r ^ 1) for r in range(reps)])

    def hop(x, mask):
        return lax.ppermute(x, "rep", [(r, r ^ (2 * mask)) for r in range(reps)])

    def meeting(j):
        found = []
        for q in range(chips):
            for c in range(2):
                for g in range(grps):
                    here = (2 * q + c) * grps + g
                    there = (2 * q + g // pair) * grps + c * pair + (g + j) % pair
                    found.append((here, there))
        return found

    def pull(x, j):
        return lax.ppermute(x, mesh_axes, [(b, a) for a, b in meeting(j)])

    def push(x, j):
        return lax.ppermute(x, mesh_axes, meeting(j))

    rounds = (grp + jnp.arange(pair)) % pair
    order = chip ^ jnp.arange(chips)

    def turn(blocks, amount):
        twice = jnp.concatenate([blocks, blocks], axis=0)
        return lax.dynamic_slice_in_dim(twice, amount % grps, grps, 0)

    def exchange(x, sign):
        return [x if j == 0 else shift(x, sign * j) for j in range(grps)]

    def own(array, index, count):
        return lax.dynamic_slice_in_dim(array, index * count, count, 0)

    def pick(array, index):
        return lax.dynamic_index_in_dim(array, index, 0, False)

    def add(terms):
        return sum(t.astype(F32) for t in terms).astype(BF)

    def spread(x):
        return [x] + [hop(x, m) for m in range(1, chips)]

    def scatter(blocks):
        mine = [lax.dynamic_index_in_dim(blocks, chip ^ m, 1, False) for m in range(chips)]
        return [mine[0]] + [hop(mine[m], m) for m in range(1, chips)]

    def to_owners(pieces):
        return [push(pick(pieces, (grp + j) % pair), j) for j in range(pair)]

    def split3(x):
        high = lax.reduce_precision(x, 8, 7)
        middle = lax.reduce_precision(x - high, 8, 7)
        return jnp.concatenate([high, middle, x - high - middle]).astype(BF)

    def total(x):
        return jnp.sum(x, axis=0, keepdims=True)

    def four(x):
        far = hop(x, 1)
        return jnp.concatenate([x, partner(x), far, partner(far)])

    def four_sum(x):
        x = x.astype(BF).reshape(4, part, width)
        far = add([x[2], partner(x[3])])
        near = x[0].astype(F32) + partner(x[1]).astype(F32)
        return near + hop(far, 1).astype(F32), far

    def line_sum(blocks):
        mine = list(lax.optimization_barrier([lax.dynamic_index_in_dim(blocks, line ^ m, 1, False) for m in range(lines)]))
        return [mine[0]] + [hop(mine[m], 2 * m) for m in range(1, lines)]

    def grp_sum(blocks):
        turned = turn(blocks, grp)
        return [turned[j] if j == 0 else shift(turned[j], j) for j in range(grps)]

    def after(x, *others):
        return lax.optimization_barrier((x, others))[0]

    cond_float = condition.astype(F32)
    cond_silu = silu_float(cond_float).astype(BF)
    cond_rows = lax.dynamic_slice_in_dim(cond_silu, grp * rows, rows, 1)
    biases = (ada_bias, qv_bias, proj_bias, fc1_bias, fc2_bias)
    small = jnp.concatenate(
        [dot(cond_rows, ada_weight), jnp.concatenate(biases).astype(F32)[None]], axis=1
    )
    heads = heads_for(qkv_weight.reshape(chips, share, 3 * width), core, grp, chip)
    fc1_mine = take_columns(fc1_weight.reshape(lines, fc1_rows, hidden_width), rank, line, grps)
    fc2_mine = own(fc2_weight, rank * lines + line, fc2_rows)
    fc_mine = jnp.concatenate([fc1_mine, fc2_mine])
    heads, small = after((heads, small), fc_mine)
    small = after(small, heads)
    small = jnp.concatenate(exchange(small, -1))
    gathered = turn(small, grps - grp)
    heads = [pull(heads[j], j) for j in range(pair)]
    mine = jnp.stack([push(latents[0], j) for j in range(pair)])
    tokens = jnp.concatenate([mine, partner(mine)]).reshape(seq, width)

    fc_quarter = lax.all_gather(fc_mine, ("grp", "rep"), axis=0, axis_index_groups=same_rank)
    fc1_quarter = fc_quarter[:, :fc1_rows].reshape(width, quarter)
    fc2_quarter = fc_quarter[:, fc1_rows:].reshape(quarter, width)

    proj_mine = after(own(proj_weight, chip, share), mine, heads, small)
    proj_pulled = [pull(proj_mine, j) for j in range(pair)]
    heads = [jnp.stack([pick(x, core) for x in heads]), jnp.stack([pick(x, 1 - core) for x in heads])]
    heads = jnp.concatenate([heads[0], partner(heads[1])])
    both_pairs = jnp.concatenate([core * pair + rounds, (1 - core) * pair + rounds])
    (qkv_heads,) = place(
        spread(heads),
        [(both_pairs[None, :] * chips + order[:, None]).reshape(-1)],
        [jax.ShapeDtypeStruct((grps * chips, share, 3 * rows), BF)],
    )
    qkv_heads = qkv_heads.reshape(width, 3 * rows)

    parts = []
    start = 6 * width
    for b in biases:
        parts.append(gathered[:, start : start + b.shape[0]])
        start += b.shape[0]
    modulation = jnp.sum(gathered[:, : 6 * width], axis=0) + parts[0].reshape(-1)
    _, scale1, gate1, shift2, scale2, gate2 = [
        modulation[None, section * width : (section + 1) * width] for section in range(6)
    ]
    qv_own = lax.dynamic_index_in_dim(parts[1].reshape(2, grps, rows), block, 1, False)
    proj_bias_whole = parts[2].reshape(1, -1)
    fc1_bias_part = lax.dynamic_index_in_dim(parts[3].reshape(grps, 4, -1), rank, 1, False).reshape(1, -1)
    fc2_bias_whole = parts[4].reshape(1, -1)

    mod1 = modulation[None, : 2 * width]
    mod1 = jnp.where(served == core, mod1, partner(mod1))
    normed_all, _ = layer_norm(tokens.astype(F32))
    adapted_all = (normed_all * (1.0 + mod1[:, width:]) + mod1[:, :width]).astype(BF)
    qkv_bias = jnp.concatenate([qv_own[:1], jnp.zeros((1, rows), F32), qv_own[1:]], axis=1)
    projected = (dot(adapted_all, qkv_heads) + qkv_bias).astype(BF)
    proj_all = spread(jnp.stack(after(proj_pulled, projected)))
    mixed, lse = attend(projected, tile)

    here, there = mixed[: seq // 2], partner(mixed[seq // 2 :])
    mixed = jnp.stack([jnp.where(core == 0, here, there), jnp.where(core == 0, there, here)])
    mixed = mixed.reshape(2, pair, part, rows)
    mixed = jnp.stack([pull(mixed[:, j], j) for j in range(pair)])
    twice = jnp.concatenate([mixed, mixed])
    mixed = lax.dynamic_slice_in_dim(twice, (pair - grp % pair) % pair, pair, 0)
    attended = mixed.reshape(grps, part, rows).transpose(1, 0, 2).reshape(part, width)

    by_hop = (rounds[None, :] * chips + order[:, None]).reshape(-1)
    proj_all = after(proj_all, mixed)
    (proj_whole,) = place(
        proj_all + [partner(x) for x in proj_all],
        [jnp.concatenate([core * pair * chips + by_hop, (1 - core) * pair * chips + by_hop])],
        [jax.ShapeDtypeStruct((grps * chips, share, width), BF)],
    )
    proj_whole = proj_whole.reshape(width, width)

    input_float = latents[0].astype(F32)
    grad_out = cotangent[0].astype(F32)
    attn_out = dot(attended, proj_whole) + proj_bias_whole
    middle = input_float + gate1 * attn_out
    normed2, inverse2 = layer_norm(middle)
    adapted2 = (normed2 * (1.0 + scale2) + shift2).astype(BF)
    grad_m = grad_out * gate2
    grad_m_b = grad_m.astype(BF)

    grad_m_four = four(grad_m_b)
    adapted_four = four(adapted2)
    grad_act = dot(grad_m_four, fc2_quarter, NT)
    hidden = dot(adapted_four, fc1_quarter) + fc1_bias_part
    activated = gelu_float(hidden).astype(BF)
    grad_h = jax.vjp(gelu_float, hidden)[1](grad_act)[0]
    grad_h_b = grad_h.astype(BF)
    grad_a2, far = four_sum(dot(grad_h_b, fc1_quarter, NT))
    adapted_four, activated, grad_m_four = after((adapted_four, activated, grad_m_four), far)
    grad_fc2 = dot(activated, grad_m_four, TN).astype(BF).reshape(grps, lines, fc2_rows, width)
    grad_fc2 = line_sum(grad_fc2)
    adapted_four = after(adapted_four, grad_fc2[0])
    grad_fc1 = dot(adapted_four, grad_h_b, TN).astype(BF)
    grad_fc1 = grad_fc1.reshape(grps, lines, fc1_rows, quarter)
    grad_fc1 = line_sum(grad_fc1)

    grad_mid = grad_out + norm_back(normed2, inverse2, grad_a2 * (1.0 + scale2))
    grad_att = grad_mid * gate1
    grad_att_b = grad_att.astype(BF)
    grad_o = dot(grad_att_b, proj_whole, NT).astype(BF)
    grad_o = grad_o.reshape(part, pair, 2, rows).transpose(1, 2, 0, 3)
    grad_o = [pick(grad_o, (grp + j) % pair) for j in range(pair)]
    mlp_out = dot(after(activated, grad_o), fc2_quarter)
    mlp_out, _ = four_sum(mlp_out)
    mlp_out = mlp_out + fc2_bias_whole
    output = middle + gate2 * mlp_out
    grad_o = jnp.stack([push(x, j) for j, x in enumerate(grad_o)], axis=1)
    grad_o = jnp.concatenate([pick(grad_o, core), partner(pick(grad_o, 1 - core))]).reshape(seq, rows)

    grad_proj = dot(attended, grad_att_b, TN).astype(BF)
    grad_proj = add([own(grad_proj, core, width // 2), partner(own(grad_proj, 1 - core, width // 2))])
    grad_proj = scatter(grad_proj.reshape(pair, chips, share, width))

    grad_fc2 = grp_sum(add(after(grad_fc2, grad_o)))
    grad_fc1 = grp_sum(add(after(grad_fc1, grad_o)))
    grad_heads, qv_sums = attend_back(projected, grad_o, lse, tile)
    grad_qkv = dot(adapted_all, grad_heads, TN).astype(BF)
    here, there = own(grad_qkv, core, width // 2), partner(own(grad_qkv, 1 - core, width // 2))
    grad_heads = after(grad_heads, here)
    grad_a1 = dot(grad_heads, qkv_heads, NT)
    mod1_sums = jnp.concatenate([total(grad_a1), total(grad_a1 * normed_all)], axis=1)
    grad_a1 = grad_a1.astype(BF)
    grad_a1 = add([grad_a1[: seq // 2], partner(grad_a1[seq // 2 :])]).reshape(pair, part, width)
    grad_a1 = sum(pull(grad_a1[j], j).astype(F32) for j in range(pair))
    fc_sums = jnp.concatenate([add(after(grad_fc1, mod1_sums)), add(after(grad_fc2, mod1_sums))])
    fc_sums = lax.all_gather(fc_sums, "rep", axis=0)
    grad_fc1_out, grad_fc2_out = place_fc(fc_sums.reshape(lines, 4, -1, width), fc1_rows, grps)

    grad_proj = add(to_owners(add(after(grad_proj, grad_heads))))
    grad_proj = add([grad_proj, partner(grad_proj)])

    normed1, inverse1 = layer_norm(input_float)
    grad_latents = grad_mid + norm_back(normed1, inverse1, grad_a1 * (1.0 + scale1))

    here, there = [x.reshape(pair, chips, share, 3 * rows) for x in (here, there)]
    grad_qkv = [
        jnp.stack([lax.dynamic_index_in_dim(x, chip ^ m, 1, False) for x in (here, there)], axis=1)
        for m in range(chips)
    ]
    grad_qkv = add([grad_qkv[0]] + [hop(grad_qkv[m], m) for m in range(1, chips)])
    grad_qkv = jnp.stack(to_owners(grad_qkv))
    grad_qkv = add([own(grad_qkv, core, pair // 2), partner(own(grad_qkv, 1 - core, pair // 2))])
    last = jnp.concatenate(
        [
            lax.dynamic_slice_in_dim(grad_proj, core * (width // 2), width // 2, 1),
            grad_qkv.transpose(2, 0, 1, 3).reshape(share, -1),
        ],
        axis=1,
    )
    last = lax.all_gather(last, "rep", axis=0)
    grad_proj_out, grad_qkv_out = place_last(last.reshape(chips, 2, share, -1), grp, pair, width)

    spread_h = lax.dynamic_update_index_in_dim(
        jnp.zeros((grps, 4, quarter // grps), F32), total(grad_h).reshape(grps, -1), rank, 1
    ).reshape(1, -1)
    spread_qv = lax.dynamic_update_index_in_dim(
        jnp.zeros((2, grps, rows), F32), qv_sums[:2], block, 1
    )
    spread_mod1 = lax.dynamic_update_index_in_dim(jnp.zeros((2, 2 * width), F32), mod1_sums, served, 0)
    sums = jnp.concatenate(
        [
            total(grad_mid * attn_out),
            total(grad_a2),
            total(grad_a2 * normed2),
            total(grad_out * mlp_out),
            spread_qv.reshape(1, -1),
            total(grad_att),
            spread_h,
            total(grad_m),
            spread_mod1.reshape(1, -1),
        ],
        axis=1,
    )
    sums = sum(exchange(sums, 1))
    sums = jnp.concatenate([sums, cond_rows.astype(F32)], axis=1)
    other = partner(sums)
    ends = sums.shape[1] - 4 * width - rows, sums.shape[1] - rows
    mod1_sums = (sums + other)[:, ends[0] : ends[1]].reshape(2, 2 * width)

    def pair_up(own_rows, other_rows, upper):
        return jnp.concatenate(
            [jnp.where(upper, other_rows, own_rows), jnp.where(upper, own_rows, other_rows)]
        )

    sums = pair_up(sums, other, core == 1)
    sums = jnp.concatenate([mod1_sums, sums[:, : ends[0]], sums[:, ends[1] :]], axis=1)
    mod_own = lax.dynamic_slice_in_dim(sums, core, 1, 0)[:, : 6 * width]
    for bit in range(1, reps.bit_length() - 1):
        other = hop(sums, 1 << (bit - 1))
        sums = pair_up(sums, other, (rep >> bit) % 2 == 1)
    grad_mod = sums[:, : 6 * width]
    cond_all = sums[:, sums.shape[1] - rows :]
    grad_ada = dot(jnp.concatenate([cond_all.astype(BF)] * 3), split3(grad_mod), TN)
    grad_silu = total(dot(split3(mod_own), ada_weight, NT))
    grad_silu = after(jnp.concatenate(exchange(grad_silu, -1)), grad_qkv)
    grad_silu = turn(grad_silu, grps - grp).reshape(1, width)
    grad_condition = jax.vjp(silu_float, cond_float)[1](grad_silu)[0]

    bias_grads = []
    summed = total(sums)[0]
    start = 0
    for b in biases:
        count = b.shape[0]
        bias_grads.append(lax.dynamic_slice_in_dim(summed, start + grp * count, count))
        start += grps * count

    return (
        output[None],
        grad_latents[None],
        grad_condition,
        grad_ada,
        bias_grads[0],
        grad_qkv_out.reshape(rows, 3 * width),
        bias_grads[1],
        grad_proj_out.reshape(rows, width),
        bias_grads[2],
        grad_fc1_out.reshape(rows, hidden_width),
        bias_grads[3],
        grad_fc2_out.reshape(-1, width),
        bias_grads[4],
    )


def solution(mesh):
    tokens, vector, matrix = P("rep", "grp", None), P("grp"), P("grp", None)
    weights = (matrix, vector) * 5
    return jax.shard_map(
        functools.partial(block_step, mesh.shape["rep"], mesh.shape["grp"]),
        mesh=mesh,
        in_specs=(tokens, P("rep", None), tokens) + weights,
        out_specs=(tokens, tokens, P("rep", None)) + weights,
        check_vma=False,
    )
```

profile of v0, /device:TPU:0, one launch (start us, length us, event | category | flops | bytes accessed | tf_op | source)
XLA Modules:
  0.0 555.2 jit_solution(2207099664539526427)
XLA Ops:
  26.0 8.8 %collective-permute-start = (f32[1,10944]{1,0:T(1,128)S(1)}, f32[1,10944]{1,0:T(1,128)S(1)}, u32[]{:S(2)}, u32[]{:S(2)}) collective-permute-start(f32[1,10944]{1,0:T(1,128)S(1)} %pad_maximum_fusion.18), channel_id=1, source_target_pairs={{0,3},{1,0},{2,1},{3,2},{4,7},{5,4},{6,5},{7,6},{8,11},{9,8},{10,9... | collective-permute-start | bytes 131336 | tf_op jit(solution)/shard_map/ppermute | solution.py:362
  35.9 34.2 %collective-permute-start.1 = (f32[1,10944]{1,0:T(1,128)S(1)}, f32[1,10944]{1,0:T(1,128)S(1)}, u32[]{:S(2)}, u32[]{:S(2)}) collective-permute-start(f32[1,10944]{1,0:T(1,128)S(1)} %pad_maximum_fusion.18), channel_id=1, source_target_pairs={{0,2},{1,3},{2,0},{3,1},{4,6},{5,7},{6,4},{7,5},{8,10},{9,11},{10,... | collective-permute-start | bytes 131336 | tf_op jit(solution)/shard_map/ppermute | solution.py:362
  70.1 4.8 collective-permute-start.2
  85.2 10.4 %collective-permute-done.10.refs_1_ = bf16[4,72,864]{2,1,0:T(8,128)(2,1)S(1)} collective-permute-done((bf16[4,72,864]{2,1,0:T(8,128)(2,1)S(1)}, bf16[4,72,864]{2,1,0:T(8,128)(2,1)S(1)}, u32[]{:S(2)}, u32[]{:S(2)}) %collective-permute-start.10) | collective-permute-done | bytes 497696 | tf_op jit(solution)/shard_map/ppermute | solution.py:368
  98.2 20.7 %collective-permute-done.11.refs_2_ = bf16[4,72,864]{2,1,0:T(8,128)(2,1)S(1)} collective-permute-done((bf16[4,72,864]{2,1,0:T(8,128)(2,1)S(1)}, bf16[4,72,864]{2,1,0:T(8,128)(2,1)S(1)}, u32[]{:S(2)}, u32[]{:S(2)}) %collective-permute-start.11) | collective-permute-done | bytes 497696 | tf_op jit(solution)/shard_map/ppermute | solution.py:368
  128.5 3.9 add_convert_fusion.2.x_ref
  132.4 14.4 %attend.1 = (bf16[1024,288]{1,0:T(8,128)(2,1)}, f32[4,1024]{1,0:T(4,128)}) custom-call(bf16[1024,864]{1,0:T(8,128)(2,1)} %add_convert_fusion.2.x_ref), custom_call_target="tpu_custom_call" | custom-call | flops 1207959552 | bytes 2359296 | tf_op jit(solution)/shard_map/attend/pallas_call | solution.py:49
  160.2 7.4 %collective-permute-done.15 = bf16[2,256,288]{2,1,0:T(8,128)(2,1)S(1)} collective-permute-done((bf16[2,256,288]{2,1,0:T(8,128)(2,1)S(1)}, bf16[2,256,288]{2,1,0:T(8,128)(2,1)S(1)}, u32[]{:S(2)}, u32[]{:S(2)}) %collective-permute-start.15) | collective-permute-done | bytes 294944 | tf_op jit(solution)/shard_map/ppermute | solution.py:381
  169.0 6.4 %collective-permute-start.21 = (bf16[2,72,1152]{2,1,0:T(8,128)(2,1)}, bf16[2,72,1152]{2,1,0:T(8,128)(2,1)S(1)}, u32[]{:S(2)}, u32[]{:S(2)}) collective-permute-start(bf16[2,72,1152]{2,1,0:T(8,128)(2,1)} %pad_maximum_fusion.12.refs_0_), channel_id=1, source_target_pairs={{0,4},{4,0},{8,12},{12,8},{16,20},{20,16},{24,28},{28,24},{1,5},{5... | collective-permute-start | bytes 995336 | tf_op jit(solution)/shard_map/ppermute | solution.py:365
  178.1 5.0 collective-permute-start.28
  184.0 3.6 place.3
  187.6 4.1 fusion.86
  195.0 3.2 pad_maximum_fusion.2
  198.5 10.6 %collective-permute-done.26 = bf16[256,1152]{1,0:T(8,128)(2,1)} collective-permute-done((bf16[256,1152]{1,0:T(8,128)(2,1)}, bf16[256,1152]{1,0:T(8,128)(2,1)}, u32[]{:S(2)}, u32[]{:S(2)}) %collective-permute-start.26) | collective-permute-done | bytes 589856 | tf_op jit(solution)/shard_map/ppermute | solution.py:368
  212.1 7.7 %multiply_convert_fusion = (bf16[1024,1152]{1,0:T(8,128)(2,1)}, f32[1024,1152]{1,0:T(8,128)S(1)}) fusion(f32[1152]{0:T(1024)S(1)} %add.564, bf16[1152,1152]{1,0:T(8,128)(2,1)S(1)} %bitcast.196, bf16[256,1152]{1,0:T(8,128)(2,1)} %collective-permute-done.27, bf16[256,1152]{1,0:T(8,128)(2,1)} %collective-permute-done.26, ...), kind=kOutput, calls=%fused_computation.15 | convolution fusion | flops 2739142656 | bytes 12096000 | tf_op jit(solution)/shard_map/dot_general | solution.py:23
  219.8 7.6 %fusion.93 = (f32[1152]{0:T(1024)S(1)}, bf16[1024,1152]{1,0:T(8,128)(2,1)S(1)}) fusion(f32[1024,1152]{1,0:T(8,128)S(1)} %get-tuple-element.213, bf16[1152,1152]{1,0:T(8,128)(2,1)S(1)} %bitcast.194, bf16[256,1152]{1,0:T(8,128)(2,1)} %collective-permute-done.30, bf16[256,1152]{1,0:T(8,128)(2,1)} %collective-permute-done.29, ...), kind=kOutput, calls=%fused_computation.300 | convolution fusion | flops 2752117760 | bytes 12096000 | tf_op jit(solution)/shard_map/dot_general | solution.py:23
  227.4 3.8 convolution_convert_fusion.4
  234.3 4.1 add_convert_fusion
  244.4 5.6 %convolution_convert_fusion.2 = bf16[1152,1152]{1,0:T(8,128)(2,1)S(1)} fusion(bf16[1024,1152]{1,0:T(8,128)(2,1)} %get-tuple-element.70, bf16[1024,1152]{1,0:T(8,128)(2,1)} %pad_maximum_fusion.2), kind=kOutput, calls=%fused_computation.2 | convolution fusion | flops 2719236096 | bytes 7372800 | tf_op jit(solution)/shard_map/dot_general | solution.py:23
  253.4 3.3 convolution_convert_fusion.1
  271.8 6.0 %convolution_convert_fusion.3 = bf16[1024,1152]{1,0:T(8,128)(2,1)S(1)} fusion(bf16[1024,1152]{1,0:T(8,128)(2,1)} %get-tuple-element.70, bf16[1152,1152]{1,0:T(8,128)(2,1)} %bitcast.195), kind=kOutput, calls=%fused_computation.20 | convolution fusion | flops 2719088640 | bytes 7372800 | tf_op jit(solution)/shard_map/dot_general | solution.py:23
  278.9 5.3 collective-permute-start.35
  292.1 21.0 %attend_back.1 = (bf16[1024,864]{1,0:T(8,128)(2,1)}, f32[8,288]{1,0:T(8,128)}) custom-call(bf16[1024,864]{1,0:T(8,128)(2,1)} %add_convert_fusion.2.x_ref, bf16[1024,288]{1,0:T(8,128)(2,1)} %bitcast.213, f32[4,1024]{1,0:T(4,128)} %get-tuple-element.71.lse_ref), custom_call_target="tpu_custom_call" | custom-call | flops 3019898880 | bytes 4128768 | tf_op jit(solution)/shard_map/attend_back/pallas_call | solution.py:110
  313.1 4.7 convolution_convert_fusion.5
  320.3 5.6 %multiply_reduce_fusion = (f32[1152]{0:T(1024)S(1)}, f32[1152]{0:T(1024)S(1)}, bf16[1024,1152]{1,0:T(8,128)(2,1)}) fusion(f32[1024]{0:T(1024)S(1)} %bitcast.222, f32[1024]{0:T(1024)S(1)} %bitcast.224, bf16[2,256,1152]{2,1,0:T(8,128)(2,1)S(1)} %collective-permute-done.5, bf16[1,256,1152]{2,1,0:T(8,128)(2,1)} %bitcast.9, ...), kind=kOutput, calls=%fused_computation.13 | convolution fusion | flops 2049046272 | bytes 8496128 | tf_op jit(solution)/shard_map/dot_general | solution.py:23
  351.5 14.4 %collective-permute-start.71 = (bf16[144,1152]{1,0:T(8,128)(2,1)S(1)}, bf16[144,1152]{1,0:T(8,128)(2,1)S(1)}, u32[]{:S(2)}, u32[]{:S(2)}) collective-permute-start(bf16[144,1152]{1,0:T(8,128)(2,1)S(1)} %get-tuple-element.148), channel_id=1, source_target_pairs={{0,1},{1,2},{2,3},{3,0},{4,5},{5,6},{6,7},{7,4},{8,9},{9,10},{10,1... | collective-permute-start | bytes 995336 | tf_op jit(solution)/shard_map/ppermute | solution.py:362
  367.8 18.7 %collective-permute-start.73 = (bf16[144,1152]{1,0:T(8,128)(2,1)S(1)}, bf16[144,1152]{1,0:T(8,128)(2,1)S(1)}, u32[]{:S(2)}, u32[]{:S(2)}) collective-permute-start(bf16[144,1152]{1,0:T(8,128)(2,1)S(1)} %get-tuple-element.146), channel_id=1, source_target_pairs={{0,3},{1,0},{2,1},{3,2},{4,7},{5,4},{6,5},{7,6},{8,11},{9,8},{10,9... | collective-permute-start | bytes 995336 | tf_op jit(solution)/shard_map/ppermute | solution.py:362
  387.4 5.9 %collective-permute-done.72 = bf16[144,1152]{1,0:T(8,128)(2,1)S(1)} collective-permute-done((bf16[144,1152]{1,0:T(8,128)(2,1)S(1)}, bf16[144,1152]{1,0:T(8,128)(2,1)S(1)}, u32[]{:S(2)}, u32[]{:S(2)}) %collective-permute-start.72) | collective-permute-done | bytes 331808 | tf_op jit(solution)/shard_map/ppermute | solution.py:362
  393.4 3.4 collective-permute-done.73
  405.9 5.8 %collective-permute-done.60 = bf16[2,72,1152]{2,1,0:T(8,128)(2,1)S(1)} collective-permute-done((bf16[2,72,1152]{2,1,0:T(8,128)(2,1)S(1)}, bf16[2,72,1152]{2,1,0:T(8,128)(2,1)S(1)}, u32[]{:S(2)}, u32[]{:S(2)}) %collective-permute-start.60) | collective-permute-done | bytes 331808 | tf_op jit(solution)/shard_map/ppermute | solution.py:368
  413.4 4.2 collective-permute-done.61
  417.6 4.4 collective-permute-start.53
  422.9 7.1 %collective-permute-done.51 = bf16[2,2,72,864]{3,2,1,0:T(8,128)(2,1)S(1)} collective-permute-done((bf16[2,2,72,864]{3,2,1,0:T(8,128)(2,1)S(1)}, bf16[2,2,72,864]{3,2,1,0:T(8,128)(2,1)S(1)}, u32[]{:S(2)}, u32[]{:S(2)}) %collective-permute-start.51) | collective-permute-done | bytes 497696 | tf_op jit(solution)/shard_map/ppermute | solution.py:368
  430.0 4.2 collective-permute-start.64
  434.2 5.7 %collective-permute-done.52 = bf16[2,2,72,864]{3,2,1,0:T(8,128)(2,1)S(1)} collective-permute-done((bf16[2,2,72,864]{3,2,1,0:T(8,128)(2,1)S(1)}, bf16[2,2,72,864]{3,2,1,0:T(8,128)(2,1)S(1)}, u32[]{:S(2)}, u32[]{:S(2)}) %collective-permute-start.52) | collective-permute-done | bytes 497696 | tf_op jit(solution)/shard_map/ppermute | solution.py:368
  442.7 4.3 collective-permute-start.55
  447.0 3.7 collective-permute-start.65
  450.8 3.3 collective-permute-done.55
  454.1 3.6 collective-permute-start.56
  457.7 3.7 collective-permute-start.43
  471.1 3.5 convolution_reduce_fusion
  474.6 5.1 collective-permute-start.47
  491.5 4.1 collective-permute-start.42
  498.3 4.5 fusion.31
  502.8 6.5 %collective-permute-done.42 = bf16[256,1152]{1,0:T(8,128)(2,1)S(1)} collective-permute-done((bf16[256,1152]{1,0:T(8,128)(2,1)S(1)}, bf16[256,1152]{1,0:T(8,128)(2,1)S(1)}, u32[]{:S(2)}, u32[]{:S(2)}) %collective-permute-start.42) | collective-permute-done | bytes 589856 | tf_op jit(solution)/shard_map/ppermute | solution.py:381
  512.0 5.5 place_last.1
  517.5 24.2 %all-gather.11.cloned.1.call-done = bf16[2304,1152]{1,0:T(8,128)(2,1)} async-done(((bf16[288,1152]{1,0:T(8,128)(2,1)}), bf16[2304,1152]{1,0:T(8,128)(2,1)}) %all-gather.11.cloned.1.call-update) | async-done | bytes 5308432 | tf_op jit(solution)/shard_map/all_gather | solution.py:573
  541.7 6.5 %place_fc.1 = (f32[2,144,4608]{2,1,0:T(8,128)}, f32[4,2,144,1152]{3,2,1,0:T(8,128)}) custom-call(bf16[2,4,288,1152]{3,2,1,0:T(8,128)(2,1)} %bitcast.185), custom_call_target="tpu_custom_call" | custom-call | bytes 15925248 | tf_op jit(solution)/shard_map/place_fc/pallas_call | solution.py:253
  (414 shorter events, 175.0 us)
Async XLA Ops:
  7.2 201.9 %all-gather.7.cloned.1.call-start = ((), (), s32[]{:S(2)}) async-start(), calls=%async_computation | async-start | bytes 5971968 | tf_op jit(solution)/shard_map/all_gather | solution.py:463
  7.2 67.8 %collective-permute-start.3 = (bf16[256,1152]{1,0:T(8,128)(2,1)}, bf16[256,1152]{1,0:T(8,128)(2,1)S(1)}, u32[]{:S(2)}, u32[]{:S(2)}) collective-permute-start(bf16[256,1152]{1,0:T(8,128)(2,1)} %bitcast.182), channel_id=1, source_target_pairs={{0,0},{1,1},{2,4},{3,5},{4,2},{5,3},{6,6},{7,7},{8,8},{9,9},{10,12... | collective-permute-start | bytes 1769480 | tf_op jit(solution)/shard_map/ppermute | solution.py:384
  9.1 66.1 %collective-permute-start.4 = (bf16[256,1152]{1,0:T(8,128)(2,1)}, bf16[256,1152]{1,0:T(8,128)(2,1)}, u32[]{:S(2)}, u32[]{:S(2)}) collective-permute-start(bf16[256,1152]{1,0:T(8,128)(2,1)} %bitcast.183), channel_id=1, source_target_pairs={{0,1},{1,0},{2,5},{3,4},{4,3},{5,2},{6,7},{7,6},{8,9},{9,8},{10,13... | collective-permute-start | bytes 1769480 | tf_op jit(solution)/shard_map/ppermute | solution.py:384
  18.5 493.6 %all-gather.9.cloned.1.call-start = ((), (), s32[]{:S(2)}) async-start(), calls=%async_computation.1 | async-start | bytes 2985984 | tf_op jit(solution)/shard_map/all_gather | solution.py:597
  25.9 44.2 %collective-permute-start.8 = (bf16[2,72,864]{2,1,0:T(8,128)(2,1)S(1)}, bf16[2,72,864]{2,1,0:T(8,128)(2,1)S(1)}, u32[]{:S(2)}, u32[]{:S(2)}) collective-permute-start(bf16[2,72,864]{2,1,0:T(8,128)(2,1)S(1)} %get-tuple-element.178), channel_id=1, source_target_pairs={{1,0},{0,1},{5,2},{4,3},{3,4},{2,5},{7,6},{6,7},{9,8},{8,9},{13,10... | collective-permute-start | bytes 746504 | tf_op jit(solution)/shard_map/ppermute | solution.py:381
  26.0 53.5 %collective-permute-start = (f32[1,10944]{1,0:T(1,128)S(1)}, f32[1,10944]{1,0:T(1,128)S(1)}, u32[]{:S(2)}, u32[]{:S(2)}) collective-permute-start(f32[1,10944]{1,0:T(1,128)S(1)} %pad_maximum_fusion.18), channel_id=1, source_target_pairs={{0,3},{1,0},{2,1},{3,2},{4,7},{5,4},{6,5},{7,6},{8,11},{9,8},{10,9... | collective-permute-start | bytes 131336 | tf_op jit(solution)/shard_map/ppermute | solution.py:362
  35.9 43.6 %collective-permute-start.1 = (f32[1,10944]{1,0:T(1,128)S(1)}, f32[1,10944]{1,0:T(1,128)S(1)}, u32[]{:S(2)}, u32[]{:S(2)}) collective-permute-start(f32[1,10944]{1,0:T(1,128)S(1)} %pad_maximum_fusion.18), channel_id=1, source_target_pairs={{0,2},{1,3},{2,0},{3,1},{4,6},{5,7},{6,4},{7,5},{8,10},{9,11},{10,... | collective-permute-start | bytes 131336 | tf_op jit(solution)/shard_map/ppermute | solution.py:362
  77.4 45.5 %collective-permute-start.5 = (bf16[2,256,1152]{2,1,0:T(8,128)(2,1)}, bf16[2,256,1152]{2,1,0:T(8,128)(2,1)S(1)}, u32[]{:S(2)}, u32[]{:S(2)}) collective-permute-start(bf16[2,256,1152]{2,1,0:T(8,128)(2,1)} %pad_maximum_fusion.3), channel_id=1, source_target_pairs={{0,4},{4,0},{8,12},{12,8},{16,20},{20,16},{24,28},{28,24},{1,5},{5... | collective-permute-start | bytes 3538952 | tf_op jit(solution)/shard_map/ppermute | solution.py:365
  80.9 14.7 %collective-permute-start.10 = (bf16[4,72,864]{2,1,0:T(8,128)(2,1)S(1)}, bf16[4,72,864]{2,1,0:T(8,128)(2,1)S(1)}, u32[]{:S(2)}, u32[]{:S(2)}) collective-permute-start(bf16[4,72,864]{2,1,0:T(8,128)(2,1)S(1)} %pad_maximum_fusion.7.refs_0_), channel_id=1, source_target_pairs={{0,8},{4,12},{8,0},{12,4},{16,24},{20,28},{24,16},{28,20},{1,9},{5... | collective-permute-start | bytes 1493000 | tf_op jit(solution)/shard_map/ppermute | solution.py:368
  82.5 36.5 %collective-permute-start.11 = (bf16[4,72,864]{2,1,0:T(8,128)(2,1)S(1)}, bf16[4,72,864]{2,1,0:T(8,128)(2,1)S(1)}, u32[]{:S(2)}, u32[]{:S(2)}) collective-permute-start(bf16[4,72,864]{2,1,0:T(8,128)(2,1)S(1)} %pad_maximum_fusion.7.refs_0_), channel_id=1, source_target_pairs={{0,16},{4,20},{8,24},{12,28},{16,0},{20,4},{24,8},{28,12},{1,17},{... | collective-permute-start | bytes 1493000 | tf_op jit(solution)/shard_map/ppermute | solution.py:368
  84.0 35.8 %collective-permute-start.12 = (bf16[4,72,864]{2,1,0:T(8,128)(2,1)S(1)}, bf16[4,72,864]{2,1,0:T(8,128)(2,1)}, u32[]{:S(2)}, u32[]{:S(2)}) collective-permute-start(bf16[4,72,864]{2,1,0:T(8,128)(2,1)S(1)} %pad_maximum_fusion.7.refs_0_), channel_id=1, source_target_pairs={{0,24},{4,28},{8,16},{12,20},{16,8},{20,12},{24,0},{28,4},{1,25},{... | collective-permute-start | bytes 1493000 | tf_op jit(solution)/shard_map/ppermute | solution.py:368
  84.5 63.4 %collective-permute-start.16 = (bf16[72,1152]{1,0:T(8,128)(2,1)S(1)}, bf16[72,1152]{1,0:T(8,128)(2,1)S(1)}, u32[]{:S(2)}, u32[]{:S(2)}) collective-permute-start(bf16[72,1152]{1,0:T(8,128)(2,1)S(1)} %constant_dynamic-slice_fusion.17), channel_id=1, source_target_pairs={{0,0},{1,1},{4,2},{5,3},{2,4},{3,5},{6,6},{7,7},{8,8},{9,9},{12,10... | collective-permute-start | bytes 497672 | tf_op jit(solution)/shard_map/ppermute | solution.py:381
  95.6 52.4 %collective-permute-start.17 = (bf16[72,1152]{1,0:T(8,128)(2,1)S(1)}, bf16[72,1152]{1,0:T(8,128)(2,1)}, u32[]{:S(2)}, u32[]{:S(2)}) collective-permute-start(bf16[72,1152]{1,0:T(8,128)(2,1)S(1)} %constant_dynamic-slice_fusion.17), channel_id=1, source_target_pairs={{1,0},{0,1},{5,2},{4,3},{3,4},{2,5},{7,6},{6,7},{9,8},{8,9},{13,10... | collective-permute-start | bytes 497672 | tf_op jit(solution)/shard_map/ppermute | solution.py:381
  150.4 17.9 %collective-permute-start.18 = (bf16[2,72,1152]{2,1,0:T(8,128)(2,1)}, bf16[2,72,1152]{2,1,0:T(8,128)(2,1)}, u32[]{:S(2)}, u32[]{:S(2)}) collective-permute-start(bf16[2,72,1152]{2,1,0:T(8,128)(2,1)} %pad_maximum_fusion.12.refs_0_), channel_id=1, source_target_pairs={{0,8},{4,12},{8,0},{12,4},{16,24},{20,28},{24,16},{28,20},{1,9},{5... | collective-permute-start | bytes 995336 | tf_op jit(solution)/shard_map/ppermute | solution.py:368
  151.0 17.4 %collective-permute-start.19 = (bf16[2,72,1152]{2,1,0:T(8,128)(2,1)}, bf16[2,72,1152]{2,1,0:T(8,128)(2,1)}, u32[]{:S(2)}, u32[]{:S(2)}) collective-permute-start(bf16[2,72,1152]{2,1,0:T(8,128)(2,1)} %pad_maximum_fusion.12.refs_0_), channel_id=1, source_target_pairs={{0,16},{4,20},{8,24},{12,28},{16,0},{20,4},{24,8},{28,12},{1,17},{... | collective-permute-start | bytes 995336 | tf_op jit(solution)/shard_map/ppermute | solution.py:368
  152.5 16.6 %collective-permute-start.20 = (bf16[2,72,1152]{2,1,0:T(8,128)(2,1)}, bf16[2,72,1152]{2,1,0:T(8,128)(2,1)}, u32[]{:S(2)}, u32[]{:S(2)}) collective-permute-start(bf16[2,72,1152]{2,1,0:T(8,128)(2,1)} %pad_maximum_fusion.12.refs_0_), channel_id=1, source_target_pairs={{0,24},{4,28},{8,16},{12,20},{16,8},{20,12},{24,0},{28,4},{1,25},{... | collective-permute-start | bytes 995336 | tf_op jit(solution)/shard_map/ppermute | solution.py:368
  159.5 18.5 %collective-permute-start.29 = (bf16[256,1152]{1,0:T(8,128)(2,1)}, bf16[256,1152]{1,0:T(8,128)(2,1)}, u32[]{:S(2)}, u32[]{:S(2)}) collective-permute-start(bf16[256,1152]{1,0:T(8,128)(2,1)} %fusion.10), channel_id=1, source_target_pairs={{0,8},{4,12},{8,0},{12,4},{16,24},{20,28},{24,16},{28,20},{1,9},{5... | collective-permute-start | bytes 1769480 | tf_op jit(solution)/shard_map/ppermute | solution.py:368
  169.0 14.1 %collective-permute-start.21 = (bf16[2,72,1152]{2,1,0:T(8,128)(2,1)}, bf16[2,72,1152]{2,1,0:T(8,128)(2,1)S(1)}, u32[]{:S(2)}, u32[]{:S(2)}) collective-permute-start(bf16[2,72,1152]{2,1,0:T(8,128)(2,1)} %pad_maximum_fusion.12.refs_0_), channel_id=1, source_target_pairs={{0,4},{4,0},{8,12},{12,8},{16,20},{20,16},{24,28},{28,24},{1,5},{5... | collective-permute-start | bytes 995336 | tf_op jit(solution)/shard_map/ppermute | solution.py:365
  178.1 17.0 %collective-permute-start.28 = (bf16[256,1152]{1,0:T(8,128)(2,1)}, bf16[256,1152]{1,0:T(8,128)(2,1)}, u32[]{:S(2)}, u32[]{:S(2)}) collective-permute-start(bf16[256,1152]{1,0:T(8,128)(2,1)} %fusion.10), channel_id=1, source_target_pairs={{0,4},{4,0},{8,12},{12,8},{16,20},{20,16},{24,28},{28,24},{1,5},{5... | collective-permute-start | bytes 1769480 | tf_op jit(solution)/shard_map/ppermute | solution.py:365
  193.2 16.0 %collective-permute-start.26 = (bf16[256,1152]{1,0:T(8,128)(2,1)}, bf16[256,1152]{1,0:T(8,128)(2,1)}, u32[]{:S(2)}, u32[]{:S(2)}) collective-permute-start(bf16[256,1152]{1,0:T(8,128)(2,1)} %add_convert_fusion.9), channel_id=1, source_target_pairs={{0,8},{4,12},{8,0},{12,4},{16,24},{20,28},{24,16},{28,20},{1,9},{5... | collective-permute-start | bytes 1769480 | tf_op jit(solution)/shard_map/ppermute | solution.py:368
  198.3 13.8 %collective-permute-start.25 = (bf16[256,1152]{1,0:T(8,128)(2,1)}, bf16[256,1152]{1,0:T(8,128)(2,1)}, u32[]{:S(2)}, u32[]{:S(2)}) collective-permute-start(bf16[256,1152]{1,0:T(8,128)(2,1)} %add_convert_fusion.9), channel_id=1, source_target_pairs={{0,4},{4,0},{8,12},{12,8},{16,20},{20,16},{24,28},{28,24},{1,5},{5... | collective-permute-start | bytes 1769480 | tf_op jit(solution)/shard_map/ppermute | solution.py:365
  241.6 19.0 %collective-permute-start.32 = (bf16[256,1152]{1,0:T(8,128)(2,1)}, bf16[256,1152]{1,0:T(8,128)(2,1)}, u32[]{:S(2)}, u32[]{:S(2)}) collective-permute-start(bf16[256,1152]{1,0:T(8,128)(2,1)} %get-tuple-element.138), channel_id=1, source_target_pairs={{0,4},{4,0},{8,12},{12,8},{16,20},{20,16},{24,28},{28,24},{1,5},{5... | collective-permute-start | bytes 1769480 | tf_op jit(solution)/shard_map/ppermute | solution.py:365
  243.6 17.0 %collective-permute-start.33 = (bf16[256,1152]{1,0:T(8,128)(2,1)S(1)}, bf16[256,1152]{1,0:T(8,128)(2,1)S(1)}, u32[]{:S(2)}, u32[]{:S(2)}) collective-permute-start(bf16[256,1152]{1,0:T(8,128)(2,1)S(1)} %add_convert_fusion.8), channel_id=1, source_target_pairs={{0,8},{4,12},{8,0},{12,4},{16,24},{20,28},{24,16},{28,20},{1,9},{5... | collective-permute-start | bytes 1769480 | tf_op jit(solution)/shard_map/ppermute | solution.py:368
  258.5 77.9 %collective-permute-start.66 = (bf16[4,144,1152]{2,1,0:T(8,128)(2,1)}, bf16[4,144,1152]{2,1,0:T(8,128)(2,1)}, u32[]{:S(2)}, u32[]{:S(2)}) collective-permute-start(bf16[4,144,1152]{2,1,0:T(8,128)(2,1)} %get-tuple-element.87), channel_id=1, source_target_pairs={{0,16},{4,20},{8,24},{12,28},{16,0},{20,4},{24,8},{28,12},{1,17},{... | collective-permute-start | bytes 3981320 | tf_op jit(solution)/shard_map/ppermute | solution.py:368
  259.9 83.1 %collective-permute-start.70 = (bf16[4,144,1152]{2,1,0:T(8,128)(2,1)}, bf16[4,144,1152]{2,1,0:T(8,128)(2,1)}, u32[]{:S(2)}, u32[]{:S(2)}) collective-permute-start(bf16[4,144,1152]{2,1,0:T(8,128)(2,1)} %get-tuple-element.94), channel_id=1, source_target_pairs={{0,16},{4,20},{8,24},{12,28},{16,0},{20,4},{24,8},{28,12},{1,17},{... | collective-permute-start | bytes 3981320 | tf_op jit(solution)/shard_map/ppermute | solution.py:368
  270.6 14.6 %collective-permute-start.37 = (bf16[2,256,288]{1,2,0:T(8,128)(2,1)S(1)}, bf16[2,256,288]{1,2,0:T(8,128)(2,1)S(1)}, u32[]{:S(2)}, u32[]{:S(2)}) collective-permute-start(bf16[2,256,288]{1,2,0:T(8,128)(2,1)S(1)} %get-tuple-element.172), channel_id=1, source_target_pairs={{0,0},{1,1},{2,4},{3,5},{4,2},{5,3},{6,6},{7,7},{8,8},{9,9},{10,12... | collective-permute-start | bytes 884744 | tf_op jit(solution)/shard_map/ppermute | solution.py:384
  271.3 15.5 %collective-permute-start.38 = (bf16[2,256,288]{1,2,0:T(8,128)(2,1)S(1)}, bf16[2,256,288]{1,2,0:T(8,128)(2,1)S(1)}, u32[]{:S(2)}, u32[]{:S(2)}) collective-permute-start(bf16[2,256,288]{1,2,0:T(8,128)(2,1)S(1)} %get-tuple-element.171), channel_id=1, source_target_pairs={{0,1},{1,0},{2,5},{3,4},{4,3},{5,2},{6,7},{7,6},{8,9},{9,8},{10,13... | collective-permute-start | bytes 884744 | tf_op jit(solution)/shard_map/ppermute | solution.py:384
  278.9 55.1 %collective-permute-start.35 = (bf16[256,1152]{1,0:T(8,128)(2,1)}, bf16[256,1152]{1,0:T(8,128)(2,1)}, u32[]{:S(2)}, u32[]{:S(2)}) collective-permute-start(bf16[256,1152]{1,0:T(8,128)(2,1)} %get-tuple-element.137), channel_id=1, source_target_pairs={{0,4},{4,0},{8,12},{12,8},{16,20},{20,16},{24,28},{28,24},{1,5},{5... | collective-permute-start | bytes 1769480 | tf_op jit(solution)/shard_map/ppermute | solution.py:365
  285.2 112.5 %collective-permute-start.34 = (bf16[256,1152]{1,0:T(8,128)(2,1)}, bf16[256,1152]{1,0:T(8,128)(2,1)}, u32[]{:S(2)}, u32[]{:S(2)}) collective-permute-start(bf16[256,1152]{1,0:T(8,128)(2,1)} %get-tuple-element.136), channel_id=1, source_target_pairs={{0,4},{4,0},{8,12},{12,8},{16,20},{20,16},{24,28},{28,24},{1,5},{5... | collective-permute-start | bytes 1769480 | tf_op jit(solution)/shard_map/ppermute | solution.py:365
  335.3 62.3 %collective-permute-start.36 = (bf16[256,1152]{1,0:T(8,128)(2,1)S(1)}, bf16[256,1152]{1,0:T(8,128)(2,1)S(1)}, u32[]{:S(2)}, u32[]{:S(2)}) collective-permute-start(bf16[256,1152]{1,0:T(8,128)(2,1)S(1)} %add_convert_fusion.7), channel_id=1, source_target_pairs={{0,8},{4,12},{8,0},{12,4},{16,24},{20,28},{24,16},{28,20},{1,9},{5... | collective-permute-start | bytes 1769480 | tf_op jit(solution)/shard_map/ppermute | solution.py:368
  338.8 12.7 %collective-permute-start.67 = (bf16[144,1152]{1,0:T(8,128)(2,1)S(1)}, bf16[144,1152]{1,0:T(8,128)(2,1)S(1)}, u32[]{:S(2)}, u32[]{:S(2)}) collective-permute-start(bf16[144,1152]{1,0:T(8,128)(2,1)S(1)} %get-tuple-element.144), channel_id=1, source_target_pairs={{0,1},{1,2},{2,3},{3,0},{4,5},{5,6},{6,7},{7,4},{8,9},{9,10},{10,1... | collective-permute-start | bytes 995336 | tf_op jit(solution)/shard_map/ppermute | solution.py:362
  341.1 24.8 %collective-permute-start.68 = (bf16[144,1152]{1,0:T(8,128)(2,1)S(1)}, bf16[144,1152]{1,0:T(8,128)(2,1)S(1)}, u32[]{:S(2)}, u32[]{:S(2)}) collective-permute-start(bf16[144,1152]{1,0:T(8,128)(2,1)S(1)} %get-tuple-element.143), channel_id=1, source_target_pairs={{0,2},{1,3},{2,0},{3,1},{4,6},{5,7},{6,4},{7,5},{8,10},{9,11},{10,... | collective-permute-start | bytes 995336 | tf_op jit(solution)/shard_map/ppermute | solution.py:362
  343.0 24.8 %collective-permute-start.69 = (bf16[144,1152]{1,0:T(8,128)(2,1)S(1)}, bf16[144,1152]{1,0:T(8,128)(2,1)S(1)}, u32[]{:S(2)}, u32[]{:S(2)}) collective-permute-start(bf16[144,1152]{1,0:T(8,128)(2,1)S(1)} %get-tuple-element.142), channel_id=1, source_target_pairs={{0,3},{1,0},{2,1},{3,2},{4,7},{5,4},{6,5},{7,6},{8,11},{9,8},{10,9... | collective-permute-start | bytes 995336 | tf_op jit(solution)/shard_map/ppermute | solution.py:362
  351.5 35.9 %collective-permute-start.71 = (bf16[144,1152]{1,0:T(8,128)(2,1)S(1)}, bf16[144,1152]{1,0:T(8,128)(2,1)S(1)}, u32[]{:S(2)}, u32[]{:S(2)}) collective-permute-start(bf16[144,1152]{1,0:T(8,128)(2,1)S(1)} %get-tuple-element.148), channel_id=1, source_target_pairs={{0,1},{1,2},{2,3},{3,0},{4,5},{5,6},{6,7},{7,4},{8,9},{9,10},{10,1... | collective-permute-start | bytes 995336 | tf_op jit(solution)/shard_map/ppermute | solution.py:362
  365.9 27.5 %collective-permute-start.72 = (bf16[144,1152]{1,0:T(8,128)(2,1)S(1)}, bf16[144,1152]{1,0:T(8,128)(2,1)S(1)}, u32[]{:S(2)}, u32[]{:S(2)}) collective-permute-start(bf16[144,1152]{1,0:T(8,128)(2,1)S(1)} %get-tuple-element.147), channel_id=1, source_target_pairs={{0,2},{1,3},{2,0},{3,1},{4,6},{5,7},{6,4},{7,5},{8,10},{9,11},{10,... | collective-permute-start | bytes 995336 | tf_op jit(solution)/shard_map/ppermute | solution.py:362
  367.8 28.9 %collective-permute-start.73 = (bf16[144,1152]{1,0:T(8,128)(2,1)S(1)}, bf16[144,1152]{1,0:T(8,128)(2,1)S(1)}, u32[]{:S(2)}, u32[]{:S(2)}) collective-permute-start(bf16[144,1152]{1,0:T(8,128)(2,1)S(1)} %get-tuple-element.146), channel_id=1, source_target_pairs={{0,3},{1,0},{2,1},{3,2},{4,7},{5,4},{6,5},{7,6},{8,11},{9,8},{10,9... | collective-permute-start | bytes 995336 | tf_op jit(solution)/shard_map/ppermute | solution.py:362
  387.4 13.1 %collective-permute-start.59 = (bf16[576,1152]{1,0:T(8,128)(2,1)S(1)}, bf16[576,1152]{1,0:T(8,128)(2,1)S(1)}, u32[]{:S(2)}, u32[]{:S(2)}) collective-permute-start(bf16[576,1152]{1,0:T(8,128)(2,1)S(1)} %copy-done.31), channel_id=1, source_target_pairs={{0,4},{4,0},{8,12},{12,8},{16,20},{20,16},{24,28},{28,24},{1,5},{5... | collective-permute-start | bytes 3981320 | tf_op jit(solution)/shard_map/ppermute | solution.py:365
  396.7 92.1 %collective-permute-start.40 = (bf16[512,1152]{1,0:T(8,128)(2,1)}, bf16[512,1152]{1,0:T(8,128)(2,1)}, u32[]{:S(2)}, u32[]{:S(2)}) collective-permute-start(bf16[512,1152]{1,0:T(8,128)(2,1)} %slice.243), channel_id=1, source_target_pairs={{0,4},{4,0},{8,12},{12,8},{16,20},{20,16},{24,28},{28,24},{1,5},{5... | collective-permute-start | bytes 3538952 | tf_op jit(solution)/shard_map/ppermute | solution.py:365
  402.0 15.6 %collective-permute-start.61 = (bf16[2,72,1152]{2,1,0:T(8,128)(2,1)S(1)}, bf16[2,72,1152]{2,1,0:T(8,128)(2,1)S(1)}, u32[]{:S(2)}, u32[]{:S(2)}) collective-permute-start(bf16[2,72,1152]{2,1,0:T(8,128)(2,1)S(1)} %get-tuple-element.151), channel_id=1, source_target_pairs={{0,16},{4,20},{8,24},{12,28},{16,0},{20,4},{24,8},{28,12},{1,17},{... | collective-permute-start | bytes 995336 | tf_op jit(solution)/shard_map/ppermute | solution.py:368
  403.2 18.8 %collective-permute-start.62 = (bf16[2,72,1152]{2,1,0:T(8,128)(2,1)S(1)}, bf16[2,72,1152]{2,1,0:T(8,128)(2,1)S(1)}, u32[]{:S(2)}, u32[]{:S(2)}) collective-permute-start(bf16[2,72,1152]{2,1,0:T(8,128)(2,1)S(1)} %get-tuple-element.150), channel_id=1, source_target_pairs={{0,24},{4,28},{8,16},{12,20},{16,8},{20,12},{24,0},{28,4},{1,25},{... | collective-permute-start | bytes 995336 | tf_op jit(solution)/shard_map/ppermute | solution.py:368
  404.7 25.2 %collective-permute-start.51 = (bf16[2,2,72,864]{3,2,1,0:T(8,128)(2,1)S(1)}, bf16[2,2,72,864]{3,2,1,0:T(8,128)(2,1)S(1)}, u32[]{:S(2)}, u32[]{:S(2)}) collective-permute-start(bf16[2,2,72,864]{3,2,1,0:T(8,128)(2,1)S(1)} %pad_maximum_fusion.8), channel_id=1, source_target_pairs={{0,8},{4,12},{8,0},{12,4},{16,24},{20,28},{24,16},{28,20},{1,9},{5... | collective-permute-start | bytes 1493000 | tf_op jit(solution)/shard_map/ppermute | solution.py:368
  411.7 28.1 %collective-permute-start.52 = (bf16[2,2,72,864]{3,2,1,0:T(8,128)(2,1)S(1)}, bf16[2,2,72,864]{3,2,1,0:T(8,128)(2,1)S(1)}, u32[]{:S(2)}, u32[]{:S(2)}) collective-permute-start(bf16[2,2,72,864]{3,2,1,0:T(8,128)(2,1)S(1)} %pad_maximum_fusion.9), channel_id=1, source_target_pairs={{0,16},{4,20},{8,24},{12,28},{16,0},{20,4},{24,8},{28,12},{1,17},{... | collective-permute-start | bytes 1493000 | tf_op jit(solution)/shard_map/ppermute | solution.py:368
  417.6 24.1 %collective-permute-start.53 = (bf16[2,2,72,864]{3,2,1,0:T(8,128)(2,1)S(1)}, bf16[2,2,72,864]{3,2,1,0:T(8,128)(2,1)S(1)}, u32[]{:S(2)}, u32[]{:S(2)}) collective-permute-start(bf16[2,2,72,864]{3,2,1,0:T(8,128)(2,1)S(1)} %pad_maximum_fusion.10), channel_id=1, source_target_pairs={{0,24},{4,28},{8,16},{12,20},{16,8},{20,12},{24,0},{28,4},{1,25},{... | collective-permute-start | bytes 1493000 | tf_op jit(solution)/shard_map/ppermute | solution.py:368
  422.2 24.7 %collective-permute-start.63 = (bf16[72,1152]{1,0:T(8,128)(2,1)S(1)}, bf16[72,1152]{1,0:T(8,128)(2,1)S(1)}, u32[]{:S(2)}, u32[]{:S(2)}) collective-permute-start(bf16[72,1152]{1,0:T(8,128)(2,1)S(1)} %get-tuple-element.181), channel_id=1, source_target_pairs={{0,0},{1,1},{2,4},{3,5},{4,2},{5,3},{6,6},{7,7},{8,8},{9,9},{10,12... | collective-permute-start | bytes 497672 | tf_op jit(solution)/shard_map/ppermute | solution.py:384
  430.0 17.0 %collective-permute-start.64 = (bf16[72,1152]{1,0:T(8,128)(2,1)S(1)}, bf16[72,1152]{1,0:T(8,128)(2,1)S(1)}, u32[]{:S(2)}, u32[]{:S(2)}) collective-permute-start(bf16[72,1152]{1,0:T(8,128)(2,1)S(1)} %get-tuple-element.182), channel_id=1, source_target_pairs={{0,1},{1,0},{2,5},{3,4},{4,3},{5,2},{6,7},{7,6},{8,9},{9,8},{10,13... | collective-permute-start | bytes 497672 | tf_op jit(solution)/shard_map/ppermute | solution.py:384
  447.0 16.3 %collective-permute-start.65 = (bf16[72,1152]{1,0:T(8,128)(2,1)S(1)}, bf16[72,1152]{1,0:T(8,128)(2,1)S(1)}, u32[]{:S(2)}, u32[]{:S(2)}) collective-permute-start(bf16[72,1152]{1,0:T(8,128)(2,1)S(1)} %add_convert_fusion.15), channel_id=1, source_target_pairs={{0,4},{4,0},{8,12},{12,8},{16,20},{20,16},{24,28},{28,24},{1,5},{5... | collective-permute-start | bytes 497672 | tf_op jit(solution)/shard_map/ppermute | solution.py:365
  467.8 73.9 %all-gather.11.cloned.1.call-start = ((), (), s32[]{:S(2)}) async-start(), calls=%async_computation.2 | async-start | bytes 5971968 | tf_op jit(solution)/shard_map/all_gather | solution.py:573
  491.5 17.8 %collective-permute-start.42 = (bf16[256,1152]{1,0:T(8,128)(2,1)S(1)}, bf16[256,1152]{1,0:T(8,128)(2,1)S(1)}, u32[]{:S(2)}, u32[]{:S(2)}) collective-permute-start(bf16[256,1152]{1,0:T(8,128)(2,1)S(1)} %get-tuple-element.155), channel_id=1, source_target_pairs={{1,0},{0,1},{5,2},{4,3},{3,4},{2,5},{7,6},{6,7},{9,8},{8,9},{13,10... | collective-permute-start | bytes 1769480 | tf_op jit(solution)/shard_map/ppermute | solution.py:381
  (79 other events, 660.1 us)
Sparse Core Ops, SparseCore 0:
  18.6 126.6 all-gather.6
  467.9 29.9 all-gather.8
  500.4 41.2 all-gather.10
where the time goes:
time: 566 us; the launch traced here: 555 us
  starting transfers between devices  186 us (33%)
  waiting for transfers between devices  129 us (23%)
  matrix products  66 us (12%)
  Pallas kernels  59.9 us (11%)
  other arithmetic  53.7 us (9%)
  local copies, waits for them, and re-layouts  45.3 us (8%)
  between operations  15.6 us (3%)
    ppermute x15, starting transfers between devices, shift(): lax.ppermute(x, 'grp', [(g, (g + amount) % grps) for g in range(grps)])  104 us
    ppermute x20, waiting for transfers between devices, hop(): return lax.ppermute(x, 'rep', [(r, r ^ 2 * mask) for r in range(reps)])  70.2 us
    dot_general x15, matrix products, dot(): return lax.dot_general(a, b, dims, preferred_element_type=F32)  66 us
    ppermute x23, starting transfers between devices, partner(): return lax.ppermute(x, 'rep', [(r, r ^ 1) for r in range(reps)])  28 us
    ppermute x20, starting transfers between devices, hop(): return lax.ppermute(x, 'rep', [(r, r ^ 2 * mask) for r in range(reps)])  25.2 us
    all_gather x1, waiting for transfers between devices, block_step(): fc_sums = lax.all_gather(fc_sums, 'rep', axis=0)  24.2 us
    pallas_call x1, Pallas kernels, attend_back(): pl.pallas_call(functools.partial(attend_back_kernel, heads, tile), grid=(...  21 us
    ppermute x8, starting transfers between devices, push(): return lax.ppermute(x, mesh_axes, meeting(j))  15.9 us
  transfers between devices with their start and end apart: 77, of which 22 were waited for; matrix products, arithmetic and copies ran while one was open for 25% of the time, Pallas kernels for 10%

commit v1 on v0

--- a/solution.py
+++ b/solution.py
@@ -6,6 +6,7 @@
 from jax import lax
 from jax.experimental import pallas as pl
 from jax.experimental.pallas import tpu as pltpu
+from jax.experimental.layout import Layout, with_layout_constraint
 from jax.sharding import PartitionSpec as P
 
 
@@ -356,7 +357,6 @@
     lines = reps // 4
     line, rank = rep // 4, rep % 4
     fc1_rows, fc2_rows = rows // lines, quarter // grps // lines
-    same_rank = [[g * reps + r for g in range(grps) for r in range(f, reps, 4)] for f in range(4)]
 
     def shift(x, amount):
         return lax.ppermute(x, "grp", [(g, (g + amount) % grps) for g in range(grps)])
@@ -417,6 +417,9 @@
         middle = lax.reduce_precision(x - high, 8, 7)
         return jnp.concatenate([high, middle, x - high - middle]).astype(BF)
 
+    def row_major(x):
+        return with_layout_constraint(x, Layout(major_to_minor=tuple(range(x.ndim))))
+
     def total(x):
         return jnp.sum(x, axis=0, keepdims=True)
 
@@ -433,6 +436,9 @@
     def line_sum(blocks):
         mine = list(lax.optimization_barrier([lax.dynamic_index_in_dim(blocks, line ^ m, 1, False) for m in range(lines)]))
         return [mine[0]] + [hop(mine[m], 2 * m) for m in range(1, lines)]
+
+    def line_spread(x):
+        return [hop(x, 2 * m) for m in range(1, lines)]
 
     def grp_sum(blocks):
         turned = turn(blocks, grp)
@@ -451,21 +457,18 @@
     heads = heads_for(qkv_weight.reshape(chips, share, 3 * width), core, grp, chip)
     fc1_mine = take_columns(fc1_weight.reshape(lines, fc1_rows, hidden_width), rank, line, grps)
     fc2_mine = own(fc2_weight, rank * lines + line, fc2_rows)
-    fc_mine = jnp.concatenate([fc1_mine, fc2_mine])
-    heads, small = after((heads, small), fc_mine)
     small = after(small, heads)
+    fc1_mine, fc2_mine = after((fc1_mine, fc2_mine), heads)
     small = jnp.concatenate(exchange(small, -1))
     gathered = turn(small, grps - grp)
     heads = [pull(heads[j], j) for j in range(pair)]
     mine = jnp.stack([push(latents[0], j) for j in range(pair)])
     tokens = jnp.concatenate([mine, partner(mine)]).reshape(seq, width)
 
-    fc_quarter = lax.all_gather(fc_mine, ("grp", "rep"), axis=0, axis_index_groups=same_rank)
-    fc1_quarter = fc_quarter[:, :fc1_rows].reshape(width, quarter)
-    fc2_quarter = fc_quarter[:, fc1_rows:].reshape(quarter, width)
-
     proj_mine = after(own(proj_weight, chip, share), mine, heads, small)
     proj_pulled = [pull(proj_mine, j) for j in range(pair)]
+    fc1_all = exchange(fc1_mine, 1)
+    fc1_own, fc2_own = line_spread(fc1_mine), line_spread(fc2_mine)
     heads = [jnp.stack([pick(x, core) for x in heads]), jnp.stack([pick(x, 1 - core) for x in heads])]
     heads = jnp.concatenate([heads[0], partner(heads[1])])
     both_pairs = jnp.concatenate([core * pair + rounds, (1 - core) * pair + rounds])
@@ -494,15 +497,18 @@
     mod1 = jnp.where(served == core, mod1, partner(mod1))
     normed_all, _ = layer_norm(tokens.astype(F32))
     adapted_all = (normed_all * (1.0 + mod1[:, width:]) + mod1[:, :width]).astype(BF)
+    adapted_all = lax.optimization_barrier(adapted_all)
     qkv_bias = jnp.concatenate([qv_own[:1], jnp.zeros((1, rows), F32), qv_own[1:]], axis=1)
     projected = (dot(adapted_all, qkv_heads) + qkv_bias).astype(BF)
     proj_all = spread(jnp.stack(after(proj_pulled, projected)))
     mixed, lse = attend(projected, tile)
 
+    fc1_all = [fc1_all[0]] + fc1_own + [z for y in after(fc1_all[1:], mixed) for z in [y] + line_spread(y)]
     here, there = mixed[: seq // 2], partner(mixed[seq // 2 :])
     mixed = jnp.stack([jnp.where(core == 0, here, there), jnp.where(core == 0, there, here)])
     mixed = mixed.reshape(2, pair, part, rows)
     mixed = jnp.stack([pull(mixed[:, j], j) for j in range(pair)])
+    fc2_all = exchange(after(fc2_mine, mixed), 1)
     twice = jnp.concatenate([mixed, mixed])
     mixed = lax.dynamic_slice_in_dim(twice, (pair - grp % pair) % pair, pair, 0)
     attended = mixed.reshape(grps, part, rows).transpose(1, 0, 2).reshape(part, width)
@@ -525,11 +531,21 @@
     grad_m = grad_out * gate2
     grad_m_b = grad_m.astype(BF)
 
+    at_grp, at_line = (grp - jnp.arange(grps)) % grps, line ^ jnp.arange(lines)
+    fc_rows_of = (at_grp[:, None] * lines + at_line[None, :]).reshape(-1)
+
+    def placed(pieces):
+        whole = jax.ShapeDtypeStruct((grps * lines, *pieces[0].shape), BF)
+        return place([x[None] for x in pieces], [fc_rows_of], [whole])[0].reshape(-1, pieces[0].shape[1])
+
+    fc1_quarter = placed(fc1_all)
+    fc2_all = [fc2_all[0]] + fc2_own + [z for y in after(fc2_all[1:], adapted2) for z in [y] + line_spread(y)]
     grad_m_four = four(grad_m_b)
     adapted_four = four(adapted2)
-    grad_act = dot(grad_m_four, fc2_quarter, NT)
     hidden = dot(adapted_four, fc1_quarter) + fc1_bias_part
     activated = gelu_float(hidden).astype(BF)
+    fc2_quarter = placed(after(fc2_all, activated))
+    grad_act = dot(grad_m_four, fc2_quarter, NT)
     grad_h = jax.vjp(gelu_float, hidden)[1](grad_act)[0]
     grad_h_b = grad_h.astype(BF)
     grad_a2, far = four_sum(dot(grad_h_b, fc1_quarter, NT))
@@ -548,22 +564,29 @@
     grad_o = grad_o.reshape(part, pair, 2, rows).transpose(1, 2, 0, 3)
     grad_o = [pick(grad_o, (grp + j) % pair) for j in range(pair)]
     mlp_out = dot(after(activated, grad_o), fc2_quarter)
+    grad_fc2 = grp_sum(add(after(grad_fc2, mlp_out)))
     mlp_out, _ = four_sum(mlp_out)
-    mlp_out = mlp_out + fc2_bias_whole
-    output = middle + gate2 * mlp_out
     grad_o = jnp.stack([push(x, j) for j, x in enumerate(grad_o)], axis=1)
     grad_o = jnp.concatenate([pick(grad_o, core), partner(pick(grad_o, 1 - core))]).reshape(seq, rows)
 
-    grad_proj = dot(attended, grad_att_b, TN).astype(BF)
-    grad_proj = add([own(grad_proj, core, width // 2), partner(own(grad_proj, 1 - core, width // 2))])
+    grad_proj = row_major(dot(attended, after(grad_att_b, grad_o), TN).astype(BF))
+    proj_here, proj_there = own(grad_proj, core, width // 2), own(grad_proj, 1 - core, width // 2)
+    proj_there = partner(proj_there)
+    grad_heads, qv_sums = attend_back(projected, grad_o, lse, tile)
+    mlp_out = after(mlp_out, grad_heads) + fc2_bias_whole
+    output = middle + gate2 * mlp_out
+    grad_fc1 = grp_sum(add(after(grad_fc1, grad_heads)))
+    grad_qkv = row_major(dot(adapted_all, grad_heads, TN).astype(BF))
+    here, there = own(grad_qkv, core, width // 2), own(grad_qkv, 1 - core, width // 2)
+    there = partner(there)
+    here, there = [x.reshape(pair, chips, share, 3 * rows) for x in (here, there)]
+    grad_qkv = [
+        jnp.stack([lax.dynamic_index_in_dim(x, chip ^ m, 1, False) for x in (here, there)], axis=1)
+        for m in range(chips)
+    ]
+    grad_heads = after(grad_heads, grad_qkv)
+    grad_proj = add(after([proj_here, proj_there], grad_qkv))
     grad_proj = scatter(grad_proj.reshape(pair, chips, share, width))
-
-    grad_fc2 = grp_sum(add(after(grad_fc2, grad_o)))
-    grad_fc1 = grp_sum(add(after(grad_fc1, grad_o)))
-    grad_heads, qv_sums = attend_back(projected, grad_o, lse, tile)
-    grad_qkv = dot(adapted_all, grad_heads, TN).astype(BF)
-    here, there = own(grad_qkv, core, width // 2), partner(own(grad_qkv, 1 - core, width // 2))
-    grad_heads = after(grad_heads, here)
     grad_a1 = dot(grad_heads, qkv_heads, NT)
     mod1_sums = jnp.concatenate([total(grad_a1), total(grad_a1 * normed_all)], axis=1)
     grad_a1 = grad_a1.astype(BF)
@@ -573,18 +596,14 @@
     fc_sums = lax.all_gather(fc_sums, "rep", axis=0)
     grad_fc1_out, grad_fc2_out = place_fc(fc_sums.reshape(lines, 4, -1, width), fc1_rows, grps)
 
-    grad_proj = add(to_owners(add(after(grad_proj, grad_heads))))
+    grad_proj = add(to_owners(add(after(grad_proj, mod1_sums))))
     grad_proj = add([grad_proj, partner(grad_proj)])
 
     normed1, inverse1 = layer_norm(input_float)
     grad_latents = grad_mid + norm_back(normed1, inverse1, grad_a1 * (1.0 + scale1))
 
-    here, there = [x.reshape(pair, chips, share, 3 * rows) for x in (here, there)]
-    grad_qkv = [
-        jnp.stack([lax.dynamic_index_in_dim(x, chip ^ m, 1, False) for x in (here, there)], axis=1)
-        for m in range(chips)
-    ]
     grad_qkv = add([grad_qkv[0]] + [hop(grad_qkv[m], m) for m in range(1, chips)])
+    qkv_sent = grad_qkv
     grad_qkv = jnp.stack(to_owners(grad_qkv))
     grad_qkv = add([own(grad_qkv, core, pair // 2), partner(own(grad_qkv, 1 - core, pair // 2))])
     last = jnp.concatenate(
@@ -618,7 +637,7 @@
         ],
         axis=1,
     )
-    sums = sum(exchange(sums, 1))
+    sums = sum(after(exchange(sums, 1), qkv_sent))
     sums = jnp.concatenate([sums, cond_rows.astype(F32)], axis=1)
     other = partner(sums)
     ends = sums.shape[1] - 4 * width - rows, sums.shape[1] - rows
@@ -639,7 +658,7 @@
     cond_all = sums[:, sums.shape[1] - rows :]
     grad_ada = dot(jnp.concatenate([cond_all.astype(BF)] * 3), split3(grad_mod), TN)
     grad_silu = total(dot(split3(mod_own), ada_weight, NT))
-    grad_silu = after(jnp.concatenate(exchange(grad_silu, -1)), grad_qkv)
+    grad_silu = jnp.concatenate(exchange(grad_silu, -1))
     grad_silu = turn(grad_silu, grps - grp).reshape(1, width)
     grad_condition = jax.vjp(silu_float, cond_float)[1](grad_silu)[0]
 

time: 566 us -> 571 us (level)
  starting transfers between devices: 186 us -> 151 us
  waiting for transfers between devices: 129 us -> 144 us
  local copies, waits for them, and re-layouts: 45.3 us -> 56.1 us
  Pallas kernels: 59.9 us -> 66.4 us
    ppermute x15 -> x21, starting transfers between devices: 104 us -> 73.8 us  [shift(): lax.ppermute(x, 'grp', [(g, (g + amount) % grps) for g in range(grps)])]
    ppermute x15 -> x21, waiting for transfers between devices: 15.9 us -> 41.3 us  [shift(): lax.ppermute(x, 'grp', [(g, (g + amount) % grps) for g in range(grps)])]
    ppermute x20 -> x28, waiting for transfers between devices: 70.2 us -> 54.6 us  [hop(): return lax.ppermute(x, 'rep', [(r, r ^ 2 * mask) for r in range(reps)])]
    ppermute x23, starting transfers between devices: 28 us -> 15.5 us  [partner(): return lax.ppermute(x, 'rep', [(r, r ^ 1) for r in range(reps)])]
    ppermute x20 -> x28, starting transfers between devices: 25.2 us -> 32.1 us  [hop(): return lax.ppermute(x, 'rep', [(r, r ^ 2 * mask) for r in range(reps)])]
    pallas_call x2 -> x4, Pallas kernels: 6.81 us -> 13.3 us  [place(): pl.pallas_call(functools.partial(place_kernel, counts, cuts), in_specs=[p...]
    unnamed x112 -> x144, local copies, waits for them, and re-layouts: 6.43 us -> 12 us
    convert_element_type x13 -> x12, other arithmetic: 10.5 us -> 15.2 us  [add(): return sum((t.astype(F32) for t in terms)).astype(BF)]
  transfers between devices with their start and end apart: 77 -> 90, of which waited for: 22 -> 26; matrix products, arithmetic and copies ran while one was open for 25% -> 29% of each run, Pallas kernels for 10% -> 10%
where the time goes in v1:
time: 571 us; the launch traced here: 561 us
  starting transfers between devices  151 us (26%)
  waiting for transfers between devices  144 us (25%)
  matrix products  68.9 us (12%)
  Pallas kernels  66.4 us (12%)
  other arithmetic  58.5 us (10%)
  local copies, waits for them, and re-layouts  56.1 us (10%)
  between operations  15.9 us (3%)
    ppermute x21, starting transfers between devices, shift(): lax.ppermute(x, 'grp', [(g, (g + amount) % grps) for g in range(grps)])  73.8 us
    dot_general x15, matrix products, dot(): return lax.dot_general(a, b, dims, preferred_element_type=F32)  68.9 us
    ppermute x28, waiting for transfers between devices, hop(): return lax.ppermute(x, 'rep', [(r, r ^ 2 * mask) for r in range(reps)])  54.6 us
    ppermute x21, waiting for transfers between devices, shift(): lax.ppermute(x, 'grp', [(g, (g + amount) % grps) for g in range(grps)])  41.3 us
    ppermute x28, starting transfers between devices, hop(): return lax.ppermute(x, 'rep', [(r, r ^ 2 * mask) for r in range(reps)])  32.1 us
    all_gather x1, waiting for transfers between devices, block_step(): fc_sums = lax.all_gather(fc_sums, 'rep', axis=0)  29.7 us
    pallas_call x1, Pallas kernels, attend_back(): pl.pallas_call(functools.partial(attend_back_kernel, heads, tile), grid=(...  20.8 us
    ppermute x8, starting transfers between devices, push(): return lax.ppermute(x, mesh_axes, meeting(j))  18.5 us
  transfers between devices with their start and end apart: 90, of which 26 were waited for; matrix products, arithmetic and copies ran while one was open for 29% of the time, Pallas kernels for 10%

profile of v1, /device:TPU:0, one launch (start us, length us, event | category | flops | bytes accessed | tf_op | source)
XLA Modules:
  0.0 561.2 jit_solution(1359391758617271464)
XLA Ops:
  17.4 3.6 collective-permute-start.7
  28.4 6.2 %collective-permute-start = (f32[1,10944]{1,0:T(1,128)S(1)}, f32[1,10944]{1,0:T(1,128)}, u32[]{:S(2)}, u32[]{:S(2)}) collective-permute-start(f32[1,10944]{1,0:T(1,128)S(1)} %pad_maximum_fusion.18), channel_id=1, source_target_pairs={{0,3},{1,0},{2,1},{3,2},{4,7},{5,4},{6,5},{7,6},{8,11},{9,8},{10,9... | collective-permute-start | bytes 131336 | tf_op jit(solution)/shard_map/ppermute | solution.py:362
  40.1 9.0 %collective-permute-start.1 = (f32[1,10944]{1,0:T(1,128)S(1)}, f32[1,10944]{1,0:T(1,128)S(1)}, u32[]{:S(2)}, u32[]{:S(2)}) collective-permute-start(f32[1,10944]{1,0:T(1,128)S(1)} %pad_maximum_fusion.18), channel_id=1, source_target_pairs={{0,2},{1,3},{2,0},{3,1},{4,6},{5,7},{6,4},{7,5},{8,10},{9,11},{10,... | collective-permute-start | bytes 131336 | tf_op jit(solution)/shard_map/ppermute | solution.py:362
  50.0 4.8 collective-permute-start.2
  69.5 9.7 %collective-permute-done.10.refs_1_ = bf16[4,72,864]{2,1,0:T(8,128)(2,1)S(1)} collective-permute-done((bf16[4,72,864]{2,1,0:T(8,128)(2,1)S(1)}, bf16[4,72,864]{2,1,0:T(8,128)(2,1)S(1)}, u32[]{:S(2)}, u32[]{:S(2)}) %collective-permute-start.10) | collective-permute-done | bytes 497696 | tf_op jit(solution)/shard_map/ppermute | solution.py:368
  80.9 10.1 %collective-permute-done.11.refs_2_ = bf16[4,72,864]{2,1,0:T(8,128)(2,1)S(1)} collective-permute-done((bf16[4,72,864]{2,1,0:T(8,128)(2,1)S(1)}, bf16[4,72,864]{2,1,0:T(8,128)(2,1)S(1)}, u32[]{:S(2)}, u32[]{:S(2)}) %collective-permute-start.11) | collective-permute-done | bytes 497696 | tf_op jit(solution)/shard_map/ppermute | solution.py:368
  98.6 3.3 add_convert_fusion
  103.4 3.9 add_convert_fusion.1.x_ref
  107.3 14.4 %attend.1 = (bf16[1024,288]{1,0:T(8,128)(2,1)}, f32[4,1024]{1,0:T(4,128)}) custom-call(bf16[1024,864]{1,0:T(8,128)(2,1)} %add_convert_fusion.1.x_ref), custom_call_target="tpu_custom_call" | custom-call | flops 1207959552 | bytes 2359296 | tf_op jit(solution)/shard_map/attend/pallas_call | solution.py:50
  133.0 7.9 %collective-permute-done.15 = bf16[2,256,288]{2,1,0:T(8,128)(2,1)S(1)} collective-permute-done((bf16[2,256,288]{2,1,0:T(8,128)(2,1)S(1)}, bf16[2,256,288]{2,1,0:T(8,128)(2,1)S(1)}, u32[]{:S(2)}, u32[]{:S(2)}) %collective-permute-start.15) | collective-permute-done | bytes 294944 | tf_op jit(solution)/shard_map/ppermute | solution.py:381
  142.4 5.8 %collective-permute-start.21 = (bf16[2,72,1152]{2,1,0:T(8,128)(2,1)S(1)}, bf16[2,72,1152]{2,1,0:T(8,128)(2,1)}, u32[]{:S(2)}, u32[]{:S(2)}) collective-permute-start(bf16[2,72,1152]{2,1,0:T(8,128)(2,1)S(1)} %pad_maximum_fusion.12.refs_0_), channel_id=1, source_target_pairs={{0,4},{4,0},{8,12},{12,8},{16,20},{20,16},{24,28},{28,24},{1,5},{5... | collective-permute-start | bytes 995336 | tf_op jit(solution)/shard_map/ppermute | solution.py:365
  149.9 4.8 collective-permute-start.29
  157.3 3.5 place.5
  160.8 3.9 fusion.87
  168.8 8.1 %collective-permute-done.30 = bf16[144,1152]{1,0:T(8,128)(2,1)} collective-permute-done((bf16[144,1152]{1,0:T(8,128)(2,1)}, bf16[144,1152]{1,0:T(8,128)(2,1)}, u32[]{:S(2)}, u32[]{:S(2)}) %collective-permute-start.30) | collective-permute-done | bytes 331808 | tf_op jit(solution)/shard_map/ppermute | solution.py:362
  178.4 7.0 %collective-permute-done.31 = bf16[144,1152]{1,0:T(8,128)(2,1)S(1)} collective-permute-done((bf16[144,1152]{1,0:T(8,128)(2,1)}, bf16[144,1152]{1,0:T(8,128)(2,1)S(1)}, u32[]{:S(2)}, u32[]{:S(2)}) %collective-permute-start.31) | collective-permute-done | bytes 331808 | tf_op jit(solution)/shard_map/ppermute | solution.py:362
  192.3 4.1 collective-permute-done.32
  196.4 6.5 %collective-permute-start.39 = (bf16[144,1152]{1,0:T(8,128)(2,1)S(1)}, bf16[144,1152]{1,0:T(8,128)(2,1)}, u32[]{:S(2)}, u32[]{:S(2)}) collective-permute-start(bf16[144,1152]{1,0:T(8,128)(2,1)S(1)} %copy-done.27), channel_id=1, source_target_pairs={{0,1},{1,2},{2,3},{3,0},{4,5},{5,6},{6,7},{7,4},{8,9},{9,10},{10,1... | collective-permute-start | bytes 995336 | tf_op jit(solution)/shard_map/ppermute | solution.py:362
  208.5 8.0 %collective-permute-start.41 = (bf16[144,1152]{1,0:T(8,128)(2,1)S(1)}, bf16[144,1152]{1,0:T(8,128)(2,1)}, u32[]{:S(2)}, u32[]{:S(2)}) collective-permute-start(bf16[144,1152]{1,0:T(8,128)(2,1)S(1)} %copy-done.27), channel_id=1, source_target_pairs={{0,3},{1,0},{2,1},{3,2},{4,7},{5,4},{6,5},{7,6},{8,11},{9,8},{10,9... | collective-permute-start | bytes 995336 | tf_op jit(solution)/shard_map/ppermute | solution.py:362
  216.6 3.2 pad_maximum_fusion.2
  219.7 3.4 place.6
  230.6 9.0 %multiply_convert_fusion = (bf16[1024,1152]{1,0:T(8,128)(2,1)}, f32[1024,1152]{1,0:T(8,128)}) fusion(f32[1152]{0:T(1024)S(1)} %add.592, bf16[1152,1152]{1,0:T(8,128)(2,1)} %bitcast.211, bf16[256,1152]{1,0:T(8,128)(2,1)} %collective-permute-done.27, bf16[256,1152]{1,0:T(8,128)(2,1)} %collective-permute-done.26, ...), kind=kOutput, calls=%fused_computation.14 | convolution fusion | flops 2739142656 | bytes 12096000 | tf_op jit(solution)/shard_map/dot_general | solution.py:24
  239.6 6.8 %collective-permute-done.43 = bf16[144,1152]{1,0:T(8,128)(2,1)} collective-permute-done((bf16[144,1152]{1,0:T(8,128)(2,1)}, bf16[144,1152]{1,0:T(8,128)(2,1)}, u32[]{:S(2)}, u32[]{:S(2)}) %collective-permute-start.43) | collective-permute-done | bytes 331808 | tf_op jit(solution)/shard_map/ppermute | solution.py:368
  246.4 5.2 collective-permute-done.44
  251.7 3.4 place.7
  255.0 9.2 %fusion.93 = (f32[1152]{0:T(1024)S(1)}, bf16[1024,1152]{1,0:T(8,128)(2,1)S(1)}) fusion(f32[1024,1152]{1,0:T(8,128)} %get-tuple-element.253, bf16[1152,1152]{1,0:T(8,128)(2,1)} %bitcast.209, bf16[256,1152]{1,0:T(8,128)(2,1)} %collective-permute-done.37, bf16[256,1152]{1,0:T(8,128)(2,1)} %collective-permute-done.36, ...), kind=kOutput, calls=%fused_computation.302 | convolution fusion | flops 2752117760 | bytes 12096000 | tf_op jit(solution)/shard_map/dot_general | solution.py:24
  264.2 3.8 convolution_convert_fusion.3
  276.3 5.0 convolution_convert_fusion.2
  283.9 3.3 convolution_convert_fusion.1
  301.4 5.9 %collective-permute-start.52 = (bf16[2,256,288]{1,2,0:T(8,128)(2,1)S(1)}, bf16[2,256,288]{1,2,0:T(8,128)(2,1)S(1)}, u32[]{:S(2)}, u32[]{:S(2)}) collective-permute-start(bf16[2,256,288]{1,2,0:T(8,128)(2,1)S(1)} %get-tuple-element.213), channel_id=1, source_target_pairs={{0,1},{1,0},{2,5},{3,4},{4,3},{5,2},{6,7},{7,6},{8,9},{9,8},{10,13... | collective-permute-start | bytes 884744 | tf_op jit(solution)/shard_map/ppermute | solution.py:384
  307.3 6.0 %fusion.94 = bf16[1024,1152]{1,0:T(8,128)(2,1)S(1)} fusion(bf16[1024,1152]{1,0:T(8,128)(2,1)} %get-tuple-element.105, bf16[1152,1152]{1,0:T(8,128)(2,1)} %bitcast.210), kind=kOutput, calls=%fused_computation.303 | convolution fusion | flops 2717908992 | bytes 7372800 | tf_op jit(solution)/shard_map/dot_general | solution.py:24
  324.7 20.8 %attend_back.1 = (bf16[1024,864]{1,0:T(8,128)(2,1)}, f32[8,288]{1,0:T(8,128)}) custom-call(bf16[1024,864]{1,0:T(8,128)(2,1)} %add_convert_fusion.1.x_ref, bf16[1024,288]{1,0:T(8,128)(2,1)} %bitcast.226, f32[4,1024]{1,0:T(4,128)} %get-tuple-element.106.lse_ref), custom_call_target="tpu_custom_call" | custom-call | flops 3019898880 | bytes 4128768 | tf_op jit(solution)/shard_map/attend_back/pallas_call | solution.py:111
  345.5 4.9 convolution_convert_fusion.4
  361.3 3.1 collective-permute-start.81
  383.4 5.6 multiply_reduce_fusion
  396.9 19.3 %collective-permute-done.86 = bf16[144,1152]{1,0:T(8,128)(2,1)} collective-permute-done((bf16[144,1152]{1,0:T(8,128)(2,1)S(1)}, bf16[144,1152]{1,0:T(8,128)(2,1)}, u32[]{:S(2)}, u32[]{:S(2)}) %collective-permute-start.86) | collective-permute-done | bytes 331808 | tf_op jit(solution)/shard_map/ppermute | solution.py:362
  418.0 6.5 %collective-permute-start.58 = (f32[1,18432]{1,0:T(1,128)}, f32[1,18432]{1,0:T(1,128)S(1)}, u32[]{:S(2)}, u32[]{:S(2)}) collective-permute-start(f32[1,18432]{1,0:T(1,128)} %constant_dynamic-update-slice_fusion.2), channel_id=1, source_target_pairs={{0,1},{1,2},{2,3},{3,0},{4,5},{5,6},{6,7},{7,4},{8,9},{9,10},{10,1... | collective-permute-start | bytes 221192 | tf_op jit(solution)/shard_map/ppermute | solution.py:362
  428.6 3.3 collective-permute-start.59
  446.9 7.1 %collective-permute-done.72 = bf16[2,72,1152]{2,1,0:T(8,128)(2,1)S(1)} collective-permute-done((bf16[2,72,1152]{2,1,0:T(8,128)(2,1)S(1)}, bf16[2,72,1152]{2,1,0:T(8,128)(2,1)S(1)}, u32[]{:S(2)}, u32[]{:S(2)}) %collective-permute-start.72) | collective-permute-done | bytes 331808 | tf_op jit(solution)/shard_map/ppermute | solution.py:368
  460.6 3.1 collective-permute-done.75
  471.7 3.3 convolution_reduce_fusion
  475.0 3.7 collective-permute-start.65
  487.6 4.6 collective-permute-done.69
  499.2 4.5 fusion.31
  503.7 6.4 %collective-permute-done.57 = bf16[256,1152]{1,0:T(8,128)(2,1)S(1)} collective-permute-done((bf16[256,1152]{1,0:T(8,128)(2,1)S(1)}, bf16[256,1152]{1,0:T(8,128)(2,1)S(1)}, u32[]{:S(2)}, u32[]{:S(2)}) %collective-permute-start.57) | collective-permute-done | bytes 589856 | tf_op jit(solution)/shard_map/ppermute | solution.py:381
  512.1 5.6 place_last.1
  517.7 29.7 %all-gather.7.cloned.1.call-done = bf16[2304,1152]{1,0:T(8,128)(2,1)} async-done(((bf16[288,1152]{1,0:T(8,128)(2,1)}), bf16[2304,1152]{1,0:T(8,128)(2,1)}) %all-gather.7.cloned.1.call-update) | async-done | bytes 5308432 | tf_op jit(solution)/shard_map/all_gather | solution.py:596
  547.4 6.5 %place_fc.1 = (f32[2,144,4608]{2,1,0:T(8,128)}, f32[4,2,144,1152]{3,2,1,0:T(8,128)}) custom-call(bf16[2,4,288,1152]{3,2,1,0:T(8,128)(2,1)} %bitcast.200), custom_call_target="tpu_custom_call" | custom-call | bytes 15925248 | tf_op jit(solution)/shard_map/place_fc/pallas_call | solution.py:254
  (475 shorter events, 219.2 us)
Async XLA Ops:
  7.3 504.9 %all-gather.5.cloned.1.call-start = ((), (), s32[]{:S(2)}) async-start(), calls=%async_computation | async-start | bytes 2985984 | tf_op jit(solution)/shard_map/all_gather | solution.py:616
  7.3 47.6 %collective-permute-start.3 = (bf16[256,1152]{1,0:T(8,128)(2,1)}, bf16[256,1152]{1,0:T(8,128)(2,1)S(1)}, u32[]{:S(2)}, u32[]{:S(2)}) collective-permute-start(bf16[256,1152]{1,0:T(8,128)(2,1)} %bitcast.198), channel_id=1, source_target_pairs={{0,0},{1,1},{2,4},{3,5},{4,2},{5,3},{6,6},{7,7},{8,8},{9,9},{10,12... | collective-permute-start | bytes 1769480 | tf_op jit(solution)/shard_map/ppermute | solution.py:384
  9.2 45.8 %collective-permute-start.4 = (bf16[256,1152]{1,0:T(8,128)(2,1)}, bf16[256,1152]{1,0:T(8,128)(2,1)}, u32[]{:S(2)}, u32[]{:S(2)}) collective-permute-start(bf16[256,1152]{1,0:T(8,128)(2,1)} %bitcast.199), channel_id=1, source_target_pairs={{0,1},{1,0},{2,5},{3,4},{4,3},{5,2},{6,7},{7,6},{8,9},{9,8},{10,13... | collective-permute-start | bytes 1769480 | tf_op jit(solution)/shard_map/ppermute | solution.py:384
  17.4 22.6 %collective-permute-start.7 = (bf16[2,72,864]{2,1,0:T(8,128)(2,1)}, bf16[2,72,864]{2,1,0:T(8,128)(2,1)}, u32[]{:S(2)}, u32[]{:S(2)}) collective-permute-start(bf16[2,72,864]{2,1,0:T(8,128)(2,1)} %get-tuple-element.219), channel_id=1, source_target_pairs={{0,0},{1,1},{4,2},{5,3},{2,4},{3,5},{6,6},{7,7},{8,8},{9,9},{12,10... | collective-permute-start | bytes 746504 | tf_op jit(solution)/shard_map/ppermute | solution.py:381
  21.0 29.0 %collective-permute-start.8 = (bf16[2,72,864]{2,1,0:T(8,128)(2,1)}, bf16[2,72,864]{2,1,0:T(8,128)(2,1)S(1)}, u32[]{:S(2)}, u32[]{:S(2)}) collective-permute-start(bf16[2,72,864]{2,1,0:T(8,128)(2,1)} %get-tuple-element.220), channel_id=1, source_target_pairs={{1,0},{0,1},{5,2},{4,3},{3,4},{2,5},{7,6},{6,7},{9,8},{8,9},{13,10... | collective-permute-start | bytes 746504 | tf_op jit(solution)/shard_map/ppermute | solution.py:381
  28.4 33.9 %collective-permute-start = (f32[1,10944]{1,0:T(1,128)S(1)}, f32[1,10944]{1,0:T(1,128)}, u32[]{:S(2)}, u32[]{:S(2)}) collective-permute-start(f32[1,10944]{1,0:T(1,128)S(1)} %pad_maximum_fusion.18), channel_id=1, source_target_pairs={{0,3},{1,0},{2,1},{3,2},{4,7},{5,4},{6,5},{7,6},{8,11},{9,8},{10,9... | collective-permute-start | bytes 131336 | tf_op jit(solution)/shard_map/ppermute | solution.py:362
  40.1 22.3 %collective-permute-start.1 = (f32[1,10944]{1,0:T(1,128)S(1)}, f32[1,10944]{1,0:T(1,128)S(1)}, u32[]{:S(2)}, u32[]{:S(2)}) collective-permute-start(f32[1,10944]{1,0:T(1,128)S(1)} %pad_maximum_fusion.18), channel_id=1, source_target_pairs={{0,2},{1,3},{2,0},{3,1},{4,6},{5,7},{6,4},{7,5},{8,10},{9,11},{10,... | collective-permute-start | bytes 131336 | tf_op jit(solution)/shard_map/ppermute | solution.py:362
  57.2 37.6 %collective-permute-start.5 = (bf16[2,256,1152]{2,1,0:T(8,128)(2,1)}, bf16[2,256,1152]{2,1,0:T(8,128)(2,1)S(1)}, u32[]{:S(2)}, u32[]{:S(2)}) collective-permute-start(bf16[2,256,1152]{2,1,0:T(8,128)(2,1)} %pad_maximum_fusion.3), channel_id=1, source_target_pairs={{0,4},{4,0},{8,12},{12,8},{16,20},{20,16},{24,28},{28,24},{1,5},{5... | collective-permute-start | bytes 3538952 | tf_op jit(solution)/shard_map/ppermute | solution.py:365
  66.1 24.9 %collective-permute-start.11 = (bf16[4,72,864]{2,1,0:T(8,128)(2,1)S(1)}, bf16[4,72,864]{2,1,0:T(8,128)(2,1)S(1)}, u32[]{:S(2)}, u32[]{:S(2)}) collective-permute-start(bf16[4,72,864]{2,1,0:T(8,128)(2,1)S(1)} %pad_maximum_fusion.6.refs_0_), channel_id=1, source_target_pairs={{0,16},{4,20},{8,24},{12,28},{16,0},{20,4},{24,8},{28,12},{1,17},{... | collective-permute-start | bytes 1493000 | tf_op jit(solution)/shard_map/ppermute | solution.py:368
  67.6 24.2 %collective-permute-start.12 = (bf16[4,72,864]{2,1,0:T(8,128)(2,1)S(1)}, bf16[4,72,864]{2,1,0:T(8,128)(2,1)}, u32[]{:S(2)}, u32[]{:S(2)}) collective-permute-start(bf16[4,72,864]{2,1,0:T(8,128)(2,1)S(1)} %pad_maximum_fusion.6.refs_0_), channel_id=1, source_target_pairs={{0,24},{4,28},{8,16},{12,20},{16,8},{20,12},{24,0},{28,4},{1,25},{... | collective-permute-start | bytes 1493000 | tf_op jit(solution)/shard_map/ppermute | solution.py:368
  68.2 54.7 %collective-permute-start.16 = (bf16[72,1152]{1,0:T(8,128)(2,1)S(1)}, bf16[72,1152]{1,0:T(8,128)(2,1)}, u32[]{:S(2)}, u32[]{:S(2)}) collective-permute-start(bf16[72,1152]{1,0:T(8,128)(2,1)S(1)} %copy-done.44), channel_id=1, source_target_pairs={{0,0},{1,1},{4,2},{5,3},{2,4},{3,5},{6,6},{7,7},{8,8},{9,9},{12,10... | collective-permute-start | bytes 497672 | tf_op jit(solution)/shard_map/ppermute | solution.py:381
  79.2 43.6 %collective-permute-start.17 = (bf16[72,1152]{1,0:T(8,128)(2,1)S(1)}, bf16[72,1152]{1,0:T(8,128)(2,1)}, u32[]{:S(2)}, u32[]{:S(2)}) collective-permute-start(bf16[72,1152]{1,0:T(8,128)(2,1)S(1)} %copy-done.44), channel_id=1, source_target_pairs={{1,0},{0,1},{5,2},{4,3},{3,4},{2,5},{7,6},{6,7},{9,8},{8,9},{13,10... | collective-permute-start | bytes 497672 | tf_op jit(solution)/shard_map/ppermute | solution.py:381
  124.0 17.6 %collective-permute-start.18 = (bf16[2,72,1152]{2,1,0:T(8,128)(2,1)S(1)}, bf16[2,72,1152]{2,1,0:T(8,128)(2,1)}, u32[]{:S(2)}, u32[]{:S(2)}) collective-permute-start(bf16[2,72,1152]{2,1,0:T(8,128)(2,1)S(1)} %pad_maximum_fusion.12.refs_0_), channel_id=1, source_target_pairs={{0,8},{4,12},{8,0},{12,4},{16,24},{20,28},{24,16},{28,20},{1,9},{5... | collective-permute-start | bytes 995336 | tf_op jit(solution)/shard_map/ppermute | solution.py:368
  132.3 17.6 %collective-permute-start.36 = (bf16[256,1152]{1,0:T(8,128)(2,1)}, bf16[256,1152]{1,0:T(8,128)(2,1)}, u32[]{:S(2)}, u32[]{:S(2)}) collective-permute-start(bf16[256,1152]{1,0:T(8,128)(2,1)} %fusion.10), channel_id=1, source_target_pairs={{0,8},{4,12},{8,0},{12,4},{16,24},{20,28},{24,16},{28,20},{1,9},{5... | collective-permute-start | bytes 1769480 | tf_op jit(solution)/shard_map/ppermute | solution.py:368
  154.7 22.1 %collective-permute-start.30 = (bf16[144,1152]{1,0:T(8,128)(2,1)}, bf16[144,1152]{1,0:T(8,128)(2,1)}, u32[]{:S(2)}, u32[]{:S(2)}) collective-permute-start(bf16[144,1152]{1,0:T(8,128)(2,1)} %take_columns.1), channel_id=1, source_target_pairs={{0,2},{1,3},{2,0},{3,1},{4,6},{5,7},{6,4},{7,5},{8,10},{9,11},{10,... | collective-permute-start | bytes 995336 | tf_op jit(solution)/shard_map/ppermute | solution.py:362
  156.8 32.5 %collective-permute-start.35 = (bf16[256,1152]{1,0:T(8,128)(2,1)}, bf16[256,1152]{1,0:T(8,128)(2,1)}, u32[]{:S(2)}, u32[]{:S(2)}) collective-permute-start(bf16[256,1152]{1,0:T(8,128)(2,1)} %fusion.10), channel_id=1, source_target_pairs={{0,4},{4,0},{8,12},{12,8},{16,20},{20,16},{24,28},{28,24},{1,5},{5... | collective-permute-start | bytes 1769480 | tf_op jit(solution)/shard_map/ppermute | solution.py:365
  156.8 33.1 %collective-permute-start.37 = (bf16[256,1152]{1,0:T(8,128)(2,1)}, bf16[256,1152]{1,0:T(8,128)(2,1)}, u32[]{:S(2)}, u32[]{:S(2)}) collective-permute-start(bf16[256,1152]{1,0:T(8,128)(2,1)} %collective-permute-done.36), channel_id=1, source_target_pairs={{0,4},{4,0},{8,12},{12,8},{16,20},{20,16},{24,28},{28,24},{1,5},{5... | collective-permute-start | bytes 1769480 | tf_op jit(solution)/shard_map/ppermute | solution.py:365
  165.2 24.7 %collective-permute-start.26 = (bf16[256,1152]{1,0:T(8,128)(2,1)S(1)}, bf16[256,1152]{1,0:T(8,128)(2,1)}, u32[]{:S(2)}, u32[]{:S(2)}) collective-permute-start(bf16[256,1152]{1,0:T(8,128)(2,1)S(1)} %add_convert_fusion.8), channel_id=1, source_target_pairs={{0,8},{4,12},{8,0},{12,4},{16,24},{20,28},{24,16},{28,20},{1,9},{5... | collective-permute-start | bytes 1769480 | tf_op jit(solution)/shard_map/ppermute | solution.py:368
  165.8 19.5 %collective-permute-start.31 = (bf16[144,1152]{1,0:T(8,128)(2,1)}, bf16[144,1152]{1,0:T(8,128)(2,1)S(1)}, u32[]{:S(2)}, u32[]{:S(2)}) collective-permute-start(bf16[144,1152]{1,0:T(8,128)(2,1)} %take_columns.1), channel_id=1, source_target_pairs={{0,3},{1,0},{2,1},{3,2},{4,7},{5,4},{6,5},{7,6},{8,11},{9,8},{10,9... | collective-permute-start | bytes 995336 | tf_op jit(solution)/shard_map/ppermute | solution.py:362
  189.3 19.2 %collective-permute-start.34 = (bf16[144,1152]{1,0:T(8,128)(2,1)S(1)}, bf16[144,1152]{1,0:T(8,128)(2,1)}, u32[]{:S(2)}, u32[]{:S(2)}) collective-permute-start(bf16[144,1152]{1,0:T(8,128)(2,1)S(1)} %collective-permute-done.31), channel_id=1, source_target_pairs={{0,16},{4,20},{8,24},{12,28},{16,0},{20,4},{24,8},{28,12},{1,17},{... | collective-permute-start | bytes 995336 | tf_op jit(solution)/shard_map/ppermute | solution.py:368
  189.9 39.3 %collective-permute-start.25 = (bf16[256,1152]{1,0:T(8,128)(2,1)S(1)}, bf16[256,1152]{1,0:T(8,128)(2,1)}, u32[]{:S(2)}, u32[]{:S(2)}) collective-permute-start(bf16[256,1152]{1,0:T(8,128)(2,1)S(1)} %add_convert_fusion.8), channel_id=1, source_target_pairs={{0,4},{4,0},{8,12},{12,8},{16,20},{20,16},{24,28},{28,24},{1,5},{5... | collective-permute-start | bytes 1769480 | tf_op jit(solution)/shard_map/ppermute | solution.py:365
  190.0 40.6 %collective-permute-start.27 = (bf16[256,1152]{1,0:T(8,128)(2,1)}, bf16[256,1152]{1,0:T(8,128)(2,1)}, u32[]{:S(2)}, u32[]{:S(2)}) collective-permute-start(bf16[256,1152]{1,0:T(8,128)(2,1)} %collective-permute-done.26), channel_id=1, source_target_pairs={{0,4},{4,0},{8,12},{12,8},{16,20},{20,16},{24,28},{28,24},{1,5},{5... | collective-permute-start | bytes 1769480 | tf_op jit(solution)/shard_map/ppermute | solution.py:365
  196.4 26.7 %collective-permute-start.39 = (bf16[144,1152]{1,0:T(8,128)(2,1)S(1)}, bf16[144,1152]{1,0:T(8,128)(2,1)}, u32[]{:S(2)}, u32[]{:S(2)}) collective-permute-start(bf16[144,1152]{1,0:T(8,128)(2,1)S(1)} %copy-done.27), channel_id=1, source_target_pairs={{0,1},{1,2},{2,3},{3,0},{4,5},{5,6},{6,7},{7,4},{8,9},{9,10},{10,1... | collective-permute-start | bytes 995336 | tf_op jit(solution)/shard_map/ppermute | solution.py:362
  203.5 22.1 %collective-permute-start.40 = (bf16[144,1152]{1,0:T(8,128)(2,1)S(1)}, bf16[144,1152]{1,0:T(8,128)(2,1)}, u32[]{:S(2)}, u32[]{:S(2)}) collective-permute-start(bf16[144,1152]{1,0:T(8,128)(2,1)S(1)} %copy-done.27), channel_id=1, source_target_pairs={{0,2},{1,3},{2,0},{3,1},{4,6},{5,7},{6,4},{7,5},{8,10},{9,11},{10,... | collective-permute-start | bytes 995336 | tf_op jit(solution)/shard_map/ppermute | solution.py:362
  208.5 18.6 %collective-permute-start.41 = (bf16[144,1152]{1,0:T(8,128)(2,1)S(1)}, bf16[144,1152]{1,0:T(8,128)(2,1)}, u32[]{:S(2)}, u32[]{:S(2)}) collective-permute-start(bf16[144,1152]{1,0:T(8,128)(2,1)S(1)} %copy-done.27), channel_id=1, source_target_pairs={{0,3},{1,0},{2,1},{3,2},{4,7},{5,4},{6,5},{7,6},{8,11},{9,8},{10,9... | collective-permute-start | bytes 995336 | tf_op jit(solution)/shard_map/ppermute | solution.py:362
  228.5 17.9 %collective-permute-start.43 = (bf16[144,1152]{1,0:T(8,128)(2,1)}, bf16[144,1152]{1,0:T(8,128)(2,1)}, u32[]{:S(2)}, u32[]{:S(2)}) collective-permute-start(bf16[144,1152]{1,0:T(8,128)(2,1)} %collective-permute-done.40), channel_id=1, source_target_pairs={{0,16},{4,20},{8,24},{12,28},{16,0},{20,4},{24,8},{28,12},{1,17},{... | collective-permute-start | bytes 995336 | tf_op jit(solution)/shard_map/ppermute | solution.py:368
  229.1 22.5 %collective-permute-start.44 = (bf16[144,1152]{1,0:T(8,128)(2,1)}, bf16[144,1152]{1,0:T(8,128)(2,1)}, u32[]{:S(2)}, u32[]{:S(2)}) collective-permute-start(bf16[144,1152]{1,0:T(8,128)(2,1)} %collective-permute-done.41), channel_id=1, source_target_pairs={{0,16},{4,20},{8,24},{12,28},{16,0},{20,4},{24,8},{28,12},{1,17},{... | collective-permute-start | bytes 995336 | tf_op jit(solution)/shard_map/ppermute | solution.py:368
  271.1 20.0 %collective-permute-start.46 = (bf16[256,1152]{1,0:T(8,128)(2,1)}, bf16[256,1152]{1,0:T(8,128)(2,1)S(1)}, u32[]{:S(2)}, u32[]{:S(2)}) collective-permute-start(bf16[256,1152]{1,0:T(8,128)(2,1)} %get-tuple-element.179), channel_id=1, source_target_pairs={{0,4},{4,0},{8,12},{12,8},{16,20},{20,16},{24,28},{28,24},{1,5},{5... | collective-permute-start | bytes 1769480 | tf_op jit(solution)/shard_map/ppermute | solution.py:365
  289.0 69.2 %collective-permute-start.80 = (bf16[4,144,1152]{2,1,0:T(8,128)(2,1)}, bf16[4,144,1152]{2,1,0:T(8,128)(2,1)}, u32[]{:S(2)}, u32[]{:S(2)}) collective-permute-start(bf16[4,144,1152]{2,1,0:T(8,128)(2,1)} %get-tuple-element.129), channel_id=1, source_target_pairs={{0,16},{4,20},{8,24},{12,28},{16,0},{20,4},{24,8},{28,12},{1,17},{... | collective-permute-start | bytes 3981320 | tf_op jit(solution)/shard_map/ppermute | solution.py:368
  290.5 74.0 %collective-permute-start.84 = (bf16[4,144,1152]{2,1,0:T(8,128)(2,1)}, bf16[4,144,1152]{2,1,0:T(8,128)(2,1)}, u32[]{:S(2)}, u32[]{:S(2)}) collective-permute-start(bf16[4,144,1152]{2,1,0:T(8,128)(2,1)} %get-tuple-element.136), channel_id=1, source_target_pairs={{0,16},{4,20},{8,24},{12,28},{16,0},{20,4},{24,8},{28,12},{1,17},{... | collective-permute-start | bytes 3981320 | tf_op jit(solution)/shard_map/ppermute | solution.py:368
  300.5 17.9 %collective-permute-start.51 = (bf16[2,256,288]{1,2,0:T(8,128)(2,1)S(1)}, bf16[2,256,288]{1,2,0:T(8,128)(2,1)S(1)}, u32[]{:S(2)}, u32[]{:S(2)}) collective-permute-start(bf16[2,256,288]{1,2,0:T(8,128)(2,1)S(1)} %get-tuple-element.214), channel_id=1, source_target_pairs={{0,0},{1,1},{2,4},{3,5},{4,2},{5,3},{6,6},{7,7},{8,8},{9,9},{10,12... | collective-permute-start | bytes 884744 | tf_op jit(solution)/shard_map/ppermute | solution.py:384
  318.5 49.6 %collective-permute-start.48 = (bf16[256,1152]{1,0:T(8,128)(2,1)}, bf16[256,1152]{1,0:T(8,128)(2,1)}, u32[]{:S(2)}, u32[]{:S(2)}) collective-permute-start(bf16[256,1152]{1,0:T(8,128)(2,1)} %get-tuple-element.177), channel_id=1, source_target_pairs={{0,4},{4,0},{8,12},{12,8},{16,20},{20,16},{24,28},{28,24},{1,5},{5... | collective-permute-start | bytes 1769480 | tf_op jit(solution)/shard_map/ppermute | solution.py:365
  320.1 50.9 %collective-permute-start.50 = (bf16[256,1152]{1,0:T(8,128)(2,1)}, bf16[256,1152]{1,0:T(8,128)(2,1)}, u32[]{:S(2)}, u32[]{:S(2)}) collective-permute-start(bf16[256,1152]{1,0:T(8,128)(2,1)} %add_convert_fusion.6), channel_id=1, source_target_pairs={{0,8},{4,12},{8,0},{12,4},{16,24},{20,28},{24,16},{28,20},{1,9},{5... | collective-permute-start | bytes 1769480 | tf_op jit(solution)/shard_map/ppermute | solution.py:368
  351.8 25.2 %collective-permute-start.54 = (bf16[576,864]{1,0:T(8,128)(2,1)}, bf16[576,864]{1,0:T(8,128)(2,1)}, u32[]{:S(2)}, u32[]{:S(2)}) collective-permute-start(bf16[576,864]{1,0:T(8,128)(2,1)} %get-tuple-element.182), channel_id=1, source_target_pairs={{0,4},{4,0},{8,12},{12,8},{16,20},{20,16},{24,28},{28,24},{1,5},{5... | collective-permute-start | bytes 2985992 | tf_op jit(solution)/shard_map/ppermute | solution.py:365
  361.3 27.7 %collective-permute-start.81 = (bf16[144,1152]{1,0:T(8,128)(2,1)S(1)}, bf16[144,1152]{1,0:T(8,128)(2,1)S(1)}, u32[]{:S(2)}, u32[]{:S(2)}) collective-permute-start(bf16[144,1152]{1,0:T(8,128)(2,1)S(1)} %get-tuple-element.185), channel_id=1, source_target_pairs={{0,1},{1,2},{2,3},{3,0},{4,5},{5,6},{6,7},{7,4},{8,9},{9,10},{10,1... | collective-permute-start | bytes 995336 | tf_op jit(solution)/shard_map/ppermute | solution.py:362
  364.5 27.0 %collective-permute-start.82 = (bf16[144,1152]{1,0:T(8,128)(2,1)S(1)}, bf16[144,1152]{1,0:T(8,128)(2,1)S(1)}, u32[]{:S(2)}, u32[]{:S(2)}) collective-permute-start(bf16[144,1152]{1,0:T(8,128)(2,1)S(1)} %get-tuple-element.184), channel_id=1, source_target_pairs={{0,2},{1,3},{2,0},{3,1},{4,6},{5,7},{6,4},{7,5},{8,10},{9,11},{10,... | collective-permute-start | bytes 995336 | tf_op jit(solution)/shard_map/ppermute | solution.py:362
  368.1 23.5 %collective-permute-start.83 = (bf16[144,1152]{1,0:T(8,128)(2,1)S(1)}, bf16[144,1152]{1,0:T(8,128)(2,1)S(1)}, u32[]{:S(2)}, u32[]{:S(2)}) collective-permute-start(bf16[144,1152]{1,0:T(8,128)(2,1)S(1)} %get-tuple-element.183), channel_id=1, source_target_pairs={{0,3},{1,0},{2,1},{3,2},{4,7},{5,4},{6,5},{7,6},{8,11},{9,8},{10,9... | collective-permute-start | bytes 995336 | tf_op jit(solution)/shard_map/ppermute | solution.py:362
  371.0 24.5 %collective-permute-start.85 = (bf16[144,1152]{1,0:T(8,128)(2,1)S(1)}, bf16[144,1152]{1,0:T(8,128)(2,1)}, u32[]{:S(2)}, u32[]{:S(2)}) collective-permute-start(bf16[144,1152]{1,0:T(8,128)(2,1)S(1)} %get-tuple-element.189), channel_id=1, source_target_pairs={{0,1},{1,2},{2,3},{3,0},{4,5},{5,6},{6,7},{7,4},{8,9},{9,10},{10,1... | collective-permute-start | bytes 995336 | tf_op jit(solution)/shard_map/ppermute | solution.py:362
  377.0 39.2 %collective-permute-start.86 = (bf16[144,1152]{1,0:T(8,128)(2,1)S(1)}, bf16[144,1152]{1,0:T(8,128)(2,1)}, u32[]{:S(2)}, u32[]{:S(2)}) collective-permute-start(bf16[144,1152]{1,0:T(8,128)(2,1)S(1)} %get-tuple-element.188), channel_id=1, source_target_pairs={{0,2},{1,3},{2,0},{3,1},{4,6},{5,7},{6,4},{7,5},{8,10},{9,11},{10,... | collective-permute-start | bytes 995336 | tf_op jit(solution)/shard_map/ppermute | solution.py:362
  389.1 28.2 %collective-permute-start.87 = (bf16[144,1152]{1,0:T(8,128)(2,1)S(1)}, bf16[144,1152]{1,0:T(8,128)(2,1)S(1)}, u32[]{:S(2)}, u32[]{:S(2)}) collective-permute-start(bf16[144,1152]{1,0:T(8,128)(2,1)S(1)} %get-tuple-element.187), channel_id=1, source_target_pairs={{0,3},{1,0},{2,1},{3,2},{4,7},{5,4},{6,5},{7,6},{8,11},{9,8},{10,9... | collective-permute-start | bytes 995336 | tf_op jit(solution)/shard_map/ppermute | solution.py:362
  391.5 37.1 %collective-permute-start.70 = (bf16[576,1152]{1,0:T(8,128)(2,1)}, bf16[576,1152]{1,0:T(8,128)(2,1)}, u32[]{:S(2)}, u32[]{:S(2)}) collective-permute-start(bf16[576,1152]{1,0:T(8,128)(2,1)} %get-tuple-element.175), channel_id=1, source_target_pairs={{0,4},{4,0},{8,12},{12,8},{16,20},{20,16},{24,28},{28,24},{1,5},{5... | collective-permute-start | bytes 3981320 | tf_op jit(solution)/shard_map/ppermute | solution.py:365
  392.2 41.5 %collective-permute-start.63 = (bf16[2,2,72,864]{3,2,1,0:T(8,128)(2,1)}, bf16[2,2,72,864]{3,2,1,0:T(8,128)(2,1)S(1)}, u32[]{:S(2)}, u32[]{:S(2)}) collective-permute-start(bf16[2,2,72,864]{3,2,1,0:T(8,128)(2,1)} %pad_maximum_fusion.10), channel_id=1, source_target_pairs={{0,24},{4,28},{8,16},{12,20},{16,8},{20,12},{24,0},{28,4},{1,25},{... | collective-permute-start | bytes 1493000 | tf_op jit(solution)/shard_map/ppermute | solution.py:368
  395.5 38.3 %collective-permute-start.62 = (bf16[2,2,72,864]{3,2,1,0:T(8,128)(2,1)}, bf16[2,2,72,864]{3,2,1,0:T(8,128)(2,1)}, u32[]{:S(2)}, u32[]{:S(2)}) collective-permute-start(bf16[2,2,72,864]{3,2,1,0:T(8,128)(2,1)} %pad_maximum_fusion.9), channel_id=1, source_target_pairs={{0,16},{4,20},{8,24},{12,28},{16,0},{20,4},{24,8},{28,12},{1,17},{... | collective-permute-start | bytes 1493000 | tf_op jit(solution)/shard_map/ppermute | solution.py:368
  416.2 17.7 %collective-permute-start.61 = (bf16[2,2,72,864]{3,2,1,0:T(8,128)(2,1)}, bf16[2,2,72,864]{3,2,1,0:T(8,128)(2,1)}, u32[]{:S(2)}, u32[]{:S(2)}) collective-permute-start(bf16[2,2,72,864]{3,2,1,0:T(8,128)(2,1)} %pad_maximum_fusion.8), channel_id=1, source_target_pairs={{0,8},{4,12},{8,0},{12,4},{16,24},{20,28},{24,16},{28,20},{1,9},{5... | collective-permute-start | bytes 1493000 | tf_op jit(solution)/shard_map/ppermute | solution.py:368
  418.0 19.5 %collective-permute-start.58 = (f32[1,18432]{1,0:T(1,128)}, f32[1,18432]{1,0:T(1,128)S(1)}, u32[]{:S(2)}, u32[]{:S(2)}) collective-permute-start(f32[1,18432]{1,0:T(1,128)} %constant_dynamic-update-slice_fusion.2), channel_id=1, source_target_pairs={{0,1},{1,2},{2,3},{3,0},{4,5},{5,6},{6,7},{7,4},{8,9},{9,10},{10,1... | collective-permute-start | bytes 221192 | tf_op jit(solution)/shard_map/ppermute | solution.py:362
  433.8 59.0 %collective-permute-start.55 = (bf16[512,1152]{1,0:T(8,128)(2,1)}, bf16[512,1152]{1,0:T(8,128)(2,1)}, u32[]{:S(2)}, u32[]{:S(2)}) collective-permute-start(bf16[512,1152]{1,0:T(8,128)(2,1)} %slice.235), channel_id=1, source_target_pairs={{0,4},{4,0},{8,12},{12,8},{16,20},{20,16},{24,28},{28,24},{1,5},{5... | collective-permute-start | bytes 3538952 | tf_op jit(solution)/shard_map/ppermute | solution.py:365
  441.2 17.3 %collective-permute-start.77 = (bf16[2,72,864]{2,1,0:T(8,128)(2,1)}, bf16[2,72,864]{2,1,0:T(8,128)(2,1)S(1)}, u32[]{:S(2)}, u32[]{:S(2)}) collective-permute-start(bf16[2,72,864]{2,1,0:T(8,128)(2,1)} %get-tuple-element.218), channel_id=1, source_target_pairs={{0,0},{1,1},{2,4},{3,5},{4,2},{5,3},{6,6},{7,7},{8,8},{9,9},{10,12... | collective-permute-start | bytes 746504 | tf_op jit(solution)/shard_map/ppermute | solution.py:384
  470.3 77.1 %all-gather.7.cloned.1.call-start = ((), (), s32[]{:S(2)}) async-start(), calls=%async_computation.1 | async-start | bytes 5971968 | tf_op jit(solution)/shard_map/all_gather | solution.py:596
  (108 other events, 1049.0 us)
Sparse Core Ops, SparseCore 0:
  470.5 33.1 all-gather.4
  506.1 41.2 all-gather.6

commit v2 on v1

--- a/solution.py
+++ b/solution.py
@@ -270,31 +270,35 @@
     )(x)
 
 
-def take_heads_kernel(pair, place_ref, x_ref, out_ref):
+def take_heads_kernel(pair, place_ref, x_ref, *out_refs):
     grp = place_ref[1]
     width = x_ref.shape[2] // 3
     rows = width // pair // 2
-    for unit in range(pair):
-        index = lax.rem(grp - unit + pair * 2, pair)
-        for core in range(2):
-            for kind in range(3):
-                start = kind * width + (2 * unit + core) * rows
-                out_ref[index, core, :, kind * rows : (kind + 1) * rows] = x_ref[0, :, start : start + rows]
+    for j, out_ref in enumerate(out_refs):
+        for unit in range(pair):
+
+            @pl.when(lax.rem(grp - j + pair * 2, pair) == unit)
+            def _():
+                for core in range(2):
+                    for kind in range(3):
+                        start = kind * width + (2 * unit + core) * rows
+                        out_ref[core, :, kind * rows : (kind + 1) * rows] = x_ref[0, :, start : start + rows]
 
 
 def heads_for(x, core, grp, chip):
     _, share, cols = x.shape
     grps = lax.axis_size("grp")
     rows = cols // 3 // grps
+    piece = jax.ShapeDtypeStruct((2, share, 3 * rows), BF)
     return pl.pallas_call(
         functools.partial(take_heads_kernel, grps // 2),
         grid_spec=pltpu.PrefetchScalarGridSpec(
             num_scalar_prefetch=1,
             grid=(1,),
             in_specs=[pl.BlockSpec((1, share, cols), lambda i, table: (table[2], 0, 0))],
-            out_specs=pl.BlockSpec((grps // 2, 2, share, 3 * rows), lambda i, table: (0, 0, 0, 0)),
+            out_specs=[pl.BlockSpec(piece.shape, lambda i, table: (0, 0, 0))] * (grps // 2),
         ),
-        out_shape=jax.ShapeDtypeStruct((grps // 2, 2, share, 3 * rows), BF),
+        out_shape=[piece] * (grps // 2),
         cost_estimate=pl.CostEstimate(flops=0, bytes_accessed=4 * share * cols, transcendentals=0),
         name="take_heads",
     )(jnp.stack([core, grp, chip]).astype(jnp.int32), x)
@@ -351,7 +355,7 @@
     chip, core = rep // 2, rep % 2
     quarter = hidden_width // 4
     mesh_axes = ("rep", "grp")
-    tile = min(256, seq)
+    tile = min(512, seq)
     served = grp // pair
     block = grp % pair * 2 + core
     lines = reps // 4
@@ -500,7 +504,7 @@
     adapted_all = lax.optimization_barrier(adapted_all)
     qkv_bias = jnp.concatenate([qv_own[:1], jnp.zeros((1, rows), F32), qv_own[1:]], axis=1)
     projected = (dot(adapted_all, qkv_heads) + qkv_bias).astype(BF)
-    proj_all = spread(jnp.stack(after(proj_pulled, projected)))
+    proj_all = spread(jnp.stack(after(proj_pulled, qkv_heads)))
     mixed, lse = attend(projected, tile)
 
     fc1_all = [fc1_all[0]] + fc1_own + [z for y in after(fc1_all[1:], mixed) for z in [y] + line_spread(y)]
@@ -514,7 +518,6 @@
     attended = mixed.reshape(grps, part, rows).transpose(1, 0, 2).reshape(part, width)
 
     by_hop = (rounds[None, :] * chips + order[:, None]).reshape(-1)
-    proj_all = after(proj_all, mixed)
     (proj_whole,) = place(
         proj_all + [partner(x) for x in proj_all],
         [jnp.concatenate([core * pair * chips + by_hop, (1 - core) * pair * chips + by_hop])],
@@ -540,7 +543,7 @@
 
     fc1_quarter = placed(fc1_all)
     fc2_all = [fc2_all[0]] + fc2_own + [z for y in after(fc2_all[1:], adapted2) for z in [y] + line_spread(y)]
-    grad_m_four = four(grad_m_b)
+    grad_m_four = lax.optimization_barrier(four(grad_m_b))
     adapted_four = four(adapted2)
     hidden = dot(adapted_four, fc1_quarter) + fc1_bias_part
     activated = gelu_float(hidden).astype(BF)
@@ -572,6 +575,8 @@
     grad_proj = row_major(dot(attended, after(grad_att_b, grad_o), TN).astype(BF))
     proj_here, proj_there = own(grad_proj, core, width // 2), own(grad_proj, 1 - core, width // 2)
     proj_there = partner(proj_there)
+    grad_proj = add([proj_here, proj_there])
+    grad_proj = scatter(grad_proj.reshape(pair, chips, share, width))
     grad_heads, qv_sums = attend_back(projected, grad_o, lse, tile)
     mlp_out = after(mlp_out, grad_heads) + fc2_bias_whole
     output = middle + gate2 * mlp_out
@@ -585,8 +590,6 @@
         for m in range(chips)
     ]
     grad_heads = after(grad_heads, grad_qkv)
-    grad_proj = add(after([proj_here, proj_there], grad_qkv))
-    grad_proj = scatter(grad_proj.reshape(pair, chips, share, width))
     grad_a1 = dot(grad_heads, qkv_heads, NT)
     mod1_sums = jnp.concatenate([total(grad_a1), total(grad_a1 * normed_all)], axis=1)
     grad_a1 = grad_a1.astype(BF)
@@ -596,7 +599,7 @@
     fc_sums = lax.all_gather(fc_sums, "rep", axis=0)
     grad_fc1_out, grad_fc2_out = place_fc(fc_sums.reshape(lines, 4, -1, width), fc1_rows, grps)
 
-    grad_proj = add(to_owners(add(after(grad_proj, mod1_sums))))
+    grad_proj = add(to_owners(add(after(grad_proj, grad_heads))))
     grad_proj = add([grad_proj, partner(grad_proj)])
 
     normed1, inverse1 = layer_norm(input_float)

time: 571 us -> 549 us (0.961)
  starting transfers between devices: 151 us -> 160 us
  waiting for transfers between devices: 144 us -> 135 us
  Pallas kernels: 66.4 us -> 59.4 us
    ppermute x23, starting transfers between devices: 15.5 us -> 38.7 us  [partner(): return lax.ppermute(x, 'rep', [(r, r ^ 1) for r in range(reps)])]
    ppermute x21, starting transfers between devices: 73.8 us -> 58.7 us  [shift(): lax.ppermute(x, 'grp', [(g, (g + amount) % grps) for g in range(grps)])]
    ppermute x8, waiting for transfers between devices: 14.3 us -> 6.62 us  [pull(): return lax.ppermute(x, mesh_axes, [(b, a) for a, b in meeting(j)])]
    ppermute x8, starting transfers between devices: 18.5 us -> 12.3 us  [push(): return lax.ppermute(x, mesh_axes, meeting(j))]
    unnamed x144 -> x130, local copies, waits for them, and re-layouts: 12 us -> 13.7 us
  transfers between devices with their start and end apart: 90 -> 90, of which waited for: 26 -> 24; matrix products, arithmetic and copies ran while one was open for 29% -> 28% of each run, Pallas kernels for 10% -> 9%
where the time goes in v2:
time: 549 us; the launch traced here: 543 us
  starting transfers between devices  160 us (29%)
  waiting for transfers between devices  135 us (25%)
  matrix products  66.3 us (12%)
  Pallas kernels  59.4 us (11%)
  other arithmetic  54 us (10%)
  local copies, waits for them, and re-layouts  53.6 us (10%)
  between operations  15.5 us (3%)
    dot_general x15, matrix products, dot(): return lax.dot_general(a, b, dims, preferred_element_type=F32)  66.3 us
    ppermute x21, starting transfers between devices, shift(): lax.ppermute(x, 'grp', [(g, (g + amount) % grps) for g in range(grps)])  58.7 us
    ppermute x28, waiting for transfers between devices, hop(): return lax.ppermute(x, 'rep', [(r, r ^ 2 * mask) for r in range(reps)])  49.3 us
    ppermute x21, waiting for transfers between devices, shift(): lax.ppermute(x, 'grp', [(g, (g + amount) % grps) for g in range(grps)])  46.8 us
    ppermute x23, starting transfers between devices, partner(): return lax.ppermute(x, 'rep', [(r, r ^ 1) for r in range(reps)])  38.7 us
    ppermute x28, starting transfers between devices, hop(): return lax.ppermute(x, 'rep', [(r, r ^ 2 * mask) for r in range(reps)])  35.2 us
    all_gather x1, waiting for transfers between devices, block_step(): fc_sums = lax.all_gather(fc_sums, 'rep', axis=0)  29 us
    pallas_call x1, Pallas kernels, attend_back(): pl.pallas_call(functools.partial(attend_back_kernel, heads, tile), grid=(...  18.2 us
  transfers between devices with their start and end apart: 90, of which 24 were waited for; matrix products, arithmetic and copies ran while one was open for 28% of the time, Pallas kernels for 9%

profile of v2, /device:TPU:0, one launch (start us, length us, event | category | flops | bytes accessed | tf_op | source)
XLA Modules:
  0.0 543.3 jit_solution(11757431216864443224)
XLA Ops:
  10.8 3.6 collective-permute-start.7
  45.7 9.5 %collective-permute-done.2 = f32[1,10944]{1,0:T(1,128)S(1)} collective-permute-done((f32[1,10944]{1,0:T(1,128)S(1)}, f32[1,10944]{1,0:T(1,128)S(1)}, u32[]{:S(2)}, u32[]{:S(2)}) %collective-permute-start.2) | collective-permute-done | bytes 43808 | tf_op jit(solution)/shard_map/ppermute | solution.py:366
  65.2 6.5 %collective-permute-done.10.refs_1_ = bf16[4,72,864]{2,1,0:T(8,128)(2,1)} collective-permute-done((bf16[4,72,864]{2,1,0:T(8,128)(2,1)S(1)}, bf16[4,72,864]{2,1,0:T(8,128)(2,1)}, u32[]{:S(2)}, u32[]{:S(2)}) %collective-permute-start.10) | collective-permute-done | bytes 497696 | tf_op jit(solution)/shard_map/ppermute | solution.py:372
  71.7 13.7 %collective-permute-done.11.refs_2_ = bf16[4,72,864]{2,1,0:T(8,128)(2,1)S(1)} collective-permute-done((bf16[4,72,864]{2,1,0:T(8,128)(2,1)S(1)}, bf16[4,72,864]{2,1,0:T(8,128)(2,1)S(1)}, u32[]{:S(2)}, u32[]{:S(2)}) %collective-permute-start.11) | collective-permute-done | bytes 497696 | tf_op jit(solution)/shard_map/ppermute | solution.py:372
  86.2 3.1 place.4
  98.9 3.9 add_convert_fusion.1.x_ref
  102.8 9.9 %attend.1 = (bf16[1024,288]{1,0:T(8,128)(2,1)}, f32[4,1024]{1,0:T(4,128)}) custom-call(bf16[1024,864]{1,0:T(8,128)(2,1)} %add_convert_fusion.1.x_ref), custom_call_target="tpu_custom_call" | custom-call | flops 1207959552 | bytes 2359296 | tf_op jit(solution)/shard_map/attend/pallas_call | solution.py:50
  120.9 3.6 collective-permute-start.15
  125.4 5.2 collective-permute-start.30
  130.6 3.5 place.5
  134.2 22.6 %collective-permute-start.37 = (bf16[256,1152]{1,0:T(8,128)(2,1)}, bf16[256,1152]{1,0:T(8,128)(2,1)}, u32[]{:S(2)}, u32[]{:S(2)}) collective-permute-start(bf16[256,1152]{1,0:T(8,128)(2,1)} %collective-permute-done.36), channel_id=1, source_target_pairs={{0,4},{4,0},{8,12},{12,8},{16,20},{20,16},{24,28},{28,24},{1,5},{5... | collective-permute-start | bytes 1769480 | tf_op jit(solution)/shard_map/ppermute | solution.py:369
  159.7 4.1 fusion.88
  168.2 6.3 %collective-permute-done.31 = bf16[144,1152]{1,0:T(8,128)(2,1)S(1)} collective-permute-done((bf16[144,1152]{1,0:T(8,128)(2,1)}, bf16[144,1152]{1,0:T(8,128)(2,1)S(1)}, u32[]{:S(2)}, u32[]{:S(2)}) %collective-permute-start.31) | collective-permute-done | bytes 331808 | tf_op jit(solution)/shard_map/ppermute | solution.py:366
  183.3 7.7 %collective-permute-start.39 = (bf16[144,1152]{1,0:T(8,128)(2,1)S(1)}, bf16[144,1152]{1,0:T(8,128)(2,1)}, u32[]{:S(2)}, u32[]{:S(2)}) collective-permute-start(bf16[144,1152]{1,0:T(8,128)(2,1)S(1)} %copy-done.33), channel_id=1, source_target_pairs={{0,1},{1,2},{2,3},{3,0},{4,5},{5,6},{6,7},{7,4},{8,9},{9,10},{10,1... | collective-permute-start | bytes 995336 | tf_op jit(solution)/shard_map/ppermute | solution.py:366
  191.0 6.0 %collective-permute-start.40 = (bf16[144,1152]{1,0:T(8,128)(2,1)S(1)}, bf16[144,1152]{1,0:T(8,128)(2,1)}, u32[]{:S(2)}, u32[]{:S(2)}) collective-permute-start(bf16[144,1152]{1,0:T(8,128)(2,1)S(1)} %copy-done.33), channel_id=1, source_target_pairs={{0,2},{1,3},{2,0},{3,1},{4,6},{5,7},{6,4},{7,5},{8,10},{9,11},{10,... | collective-permute-start | bytes 995336 | tf_op jit(solution)/shard_map/ppermute | solution.py:366
  197.6 4.3 collective-permute-start.41
  201.9 3.2 pad_maximum_fusion.2
  205.1 3.4 place.6
  212.9 4.7 collective-permute-done.41
  221.2 9.0 %multiply_convert_fusion = (bf16[1024,1152]{1,0:T(8,128)(2,1)}, f32[1024,1152]{1,0:T(8,128)}) fusion(f32[1152]{0:T(1024)S(1)} %add.592, bf16[1152,1152]{1,0:T(8,128)(2,1)} %bitcast.213, bf16[256,1152]{1,0:T(8,128)(2,1)} %collective-permute-done.27, bf16[256,1152]{1,0:T(8,128)(2,1)} %collective-permute-done.26, ...), kind=kOutput, calls=%fused_computation.14 | convolution fusion | flops 2739142656 | bytes 12096000 | tf_op jit(solution)/shard_map/dot_general | solution.py:24
  230.3 5.5 %collective-permute-done.43 = bf16[144,1152]{1,0:T(8,128)(2,1)} collective-permute-done((bf16[144,1152]{1,0:T(8,128)(2,1)}, bf16[144,1152]{1,0:T(8,128)(2,1)}, u32[]{:S(2)}, u32[]{:S(2)}) %collective-permute-start.43) | collective-permute-done | bytes 331808 | tf_op jit(solution)/shard_map/ppermute | solution.py:372
  235.8 5.6 %collective-permute-done.44 = bf16[144,1152]{1,0:T(8,128)(2,1)} collective-permute-done((bf16[144,1152]{1,0:T(8,128)(2,1)}, bf16[144,1152]{1,0:T(8,128)(2,1)}, u32[]{:S(2)}, u32[]{:S(2)}) %collective-permute-start.44) | collective-permute-done | bytes 331808 | tf_op jit(solution)/shard_map/ppermute | solution.py:372
  241.3 3.4 place.7
  244.7 8.6 %fusion.84 = (f32[1152]{0:T(1024)S(1)}, bf16[1024,1152]{1,0:T(8,128)(2,1)S(1)}) fusion(f32[1024,1152]{1,0:T(8,128)} %get-tuple-element.243, bf16[1024,1152]{1,0:T(8,128)(2,1)} %pad_maximum_fusion.2, bf16[1152,1152]{1,0:T(8,128)(2,1)} %bitcast.211), kind=kOutput, calls=%fused_computation.291 | convolution fusion | flops 2742680576 | bytes 12096000 | tf_op jit(solution)/shard_map/dot_general | solution.py:24
  253.3 3.8 convolution_convert_fusion.3
  265.1 5.0 convolution_convert_fusion.2
  272.7 3.3 convolution_convert_fusion.1
  289.5 3.4 collective-permute-start.52
  292.9 6.0 %fusion.94 = bf16[1024,1152]{1,0:T(8,128)(2,1)S(1)} fusion(bf16[1024,1152]{1,0:T(8,128)(2,1)} %get-tuple-element.99, bf16[1152,1152]{1,0:T(8,128)(2,1)} %bitcast.212), kind=kOutput, calls=%fused_computation.299 | convolution fusion | flops 2717908992 | bytes 7372800 | tf_op jit(solution)/shard_map/dot_general | solution.py:24
  299.9 3.1 collective-permute-start.49
  309.0 18.2 %attend_back.1 = (bf16[1024,864]{1,0:T(8,128)(2,1)}, f32[8,288]{1,0:T(8,128)}) custom-call(bf16[1024,864]{1,0:T(8,128)(2,1)} %add_convert_fusion.1.x_ref, bf16[1024,288]{1,0:T(8,128)(2,1)} %bitcast.228, f32[4,1024]{1,0:T(4,128)} %get-tuple-element.100.lse_ref), custom_call_target="tpu_custom_call" | custom-call | flops 3019898880 | bytes 4128768 | tf_op jit(solution)/shard_map/attend_back/pallas_call | solution.py:111
  327.2 4.9 convolution_convert_fusion.4
  343.6 3.6 collective-permute-start.81
  366.8 4.6 multiply_reduce_fusion
  371.4 3.2 collective-permute-start.87
  379.2 19.4 %collective-permute-done.86 = bf16[144,1152]{1,0:T(8,128)(2,1)} collective-permute-done((bf16[144,1152]{1,0:T(8,128)(2,1)S(1)}, bf16[144,1152]{1,0:T(8,128)(2,1)}, u32[]{:S(2)}, u32[]{:S(2)}) %collective-permute-start.86) | collective-permute-done | bytes 331808 | tf_op jit(solution)/shard_map/ppermute | solution.py:366
  400.4 8.1 %collective-permute-start.58 = (f32[1,18432]{1,0:T(1,128)}, f32[1,18432]{1,0:T(1,128)S(1)}, u32[]{:S(2)}, u32[]{:S(2)}) collective-permute-start(f32[1,18432]{1,0:T(1,128)} %constant_dynamic-update-slice_fusion.2), channel_id=1, source_target_pairs={{0,1},{1,2},{2,3},{3,0},{4,5},{5,6},{6,7},{7,4},{8,9},{9,10},{10,1... | collective-permute-start | bytes 221192 | tf_op jit(solution)/shard_map/ppermute | solution.py:366
  414.6 3.5 collective-permute-start.59
  427.0 3.7 collective-permute-done.71
  432.7 7.6 %collective-permute-done.72 = bf16[2,72,1152]{2,1,0:T(8,128)(2,1)S(1)} collective-permute-done((bf16[2,72,1152]{2,1,0:T(8,128)(2,1)S(1)}, bf16[2,72,1152]{2,1,0:T(8,128)(2,1)S(1)}, u32[]{:S(2)}, u32[]{:S(2)}) %collective-permute-start.72) | collective-permute-done | bytes 331808 | tf_op jit(solution)/shard_map/ppermute | solution.py:372
  454.8 3.3 convolution_reduce_fusion
  458.1 3.7 collective-permute-start.65
  470.4 4.9 collective-permute-done.69
  482.0 4.5 fusion.31
  486.5 6.6 %collective-permute-done.57 = bf16[256,1152]{1,0:T(8,128)(2,1)S(1)} collective-permute-done((bf16[256,1152]{1,0:T(8,128)(2,1)S(1)}, bf16[256,1152]{1,0:T(8,128)(2,1)S(1)}, u32[]{:S(2)}, u32[]{:S(2)}) %collective-permute-start.57) | collective-permute-done | bytes 589856 | tf_op jit(solution)/shard_map/ppermute | solution.py:385
  495.1 5.6 %place_last.1 = (f32[4,72,1152]{2,1,0:T(8,128)}, f32[4,72,3456]{2,1,0:T(8,128)}) custom-call(s32[1]{0:T(128)} %bitcast.2.place_ref, bf16[4,2,72,2304]{3,2,1,0:T(8,128)(2,1)} %bitcast.210), custom_call_target="tpu_custom_call" | custom-call | bytes 7962624 | tf_op jit(solution)/shard_map/place_last/pallas_call | solution.py:191
  500.7 29.0 %all-gather.7.cloned.1.call-done = bf16[2304,1152]{1,0:T(8,128)(2,1)} async-done(((bf16[288,1152]{1,0:T(8,128)(2,1)}), bf16[2304,1152]{1,0:T(8,128)(2,1)}) %all-gather.7.cloned.1.call-update) | async-done | bytes 5308432 | tf_op jit(solution)/shard_map/all_gather | solution.py:599
  529.7 6.5 %place_fc.1 = (f32[2,144,4608]{2,1,0:T(8,128)}, f32[4,2,144,1152]{3,2,1,0:T(8,128)}) custom-call(bf16[2,4,288,1152]{3,2,1,0:T(8,128)(2,1)} %bitcast.202), custom_call_target="tpu_custom_call" | custom-call | bytes 15925248 | tf_op jit(solution)/shard_map/place_fc/pallas_call | solution.py:254
  (460 shorter events, 205.7 us)
Async XLA Ops:
  7.2 487.9 %all-gather.5.cloned.1.call-start = ((), (), s32[]{:S(2)}) async-start(), calls=%async_computation | async-start | bytes 2985984 | tf_op jit(solution)/shard_map/all_gather | solution.py:619
  10.8 24.2 %collective-permute-start.7 = (bf16[2,72,864]{2,1,0:T(8,128)(2,1)}, bf16[2,72,864]{2,1,0:T(8,128)(2,1)}, u32[]{:S(2)}, u32[]{:S(2)}) collective-permute-start(bf16[2,72,864]{2,1,0:T(8,128)(2,1)} %get-tuple-element.75), channel_id=1, source_target_pairs={{0,0},{1,1},{4,2},{5,3},{2,4},{3,5},{6,6},{7,7},{8,8},{9,9},{12,10... | collective-permute-start | bytes 746504 | tf_op jit(solution)/shard_map/ppermute | solution.py:385
  14.4 22.8 %collective-permute-start.8 = (bf16[2,72,864]{2,1,0:T(8,128)(2,1)}, bf16[2,72,864]{2,1,0:T(8,128)(2,1)S(1)}, u32[]{:S(2)}, u32[]{:S(2)}) collective-permute-start(bf16[2,72,864]{2,1,0:T(8,128)(2,1)} %get-tuple-element.76), channel_id=1, source_target_pairs={{1,0},{0,1},{5,2},{4,3},{3,4},{2,5},{7,6},{6,7},{9,8},{8,9},{13,10... | collective-permute-start | bytes 746504 | tf_op jit(solution)/shard_map/ppermute | solution.py:385
  28.9 29.6 %collective-permute-start.3 = (bf16[256,1152]{1,0:T(8,128)(2,1)}, bf16[256,1152]{1,0:T(8,128)(2,1)S(1)}, u32[]{:S(2)}, u32[]{:S(2)}) collective-permute-start(bf16[256,1152]{1,0:T(8,128)(2,1)} %bitcast.200), channel_id=1, source_target_pairs={{0,0},{1,1},{2,4},{3,5},{4,2},{5,3},{6,6},{7,7},{8,8},{9,9},{10,12... | collective-permute-start | bytes 1769480 | tf_op jit(solution)/shard_map/ppermute | solution.py:388
  35.0 23.6 %collective-permute-start.4 = (bf16[256,1152]{1,0:T(8,128)(2,1)}, bf16[256,1152]{1,0:T(8,128)(2,1)S(1)}, u32[]{:S(2)}, u32[]{:S(2)}) collective-permute-start(bf16[256,1152]{1,0:T(8,128)(2,1)} %bitcast.201), channel_id=1, source_target_pairs={{0,1},{1,0},{2,5},{3,4},{4,3},{5,2},{6,7},{7,6},{8,9},{9,8},{10,13... | collective-permute-start | bytes 1769480 | tf_op jit(solution)/shard_map/ppermute | solution.py:388
  37.3 19.5 %collective-permute-start.9 = (bf16[2,72,864]{2,1,0:T(8,128)(2,1)S(1)}, bf16[2,72,864]{2,1,0:T(8,128)(2,1)S(1)}, u32[]{:S(2)}, u32[]{:S(2)}) collective-permute-start(bf16[2,72,864]{2,1,0:T(8,128)(2,1)S(1)} %pad_maximum_fusion.15), channel_id=1, source_target_pairs={{0,4},{4,0},{8,12},{12,8},{16,20},{20,16},{24,28},{28,24},{1,5},{5... | collective-permute-start | bytes 746504 | tf_op jit(solution)/shard_map/ppermute | solution.py:369
  59.7 34.2 %collective-permute-start.5 = (bf16[2,256,1152]{2,1,0:T(8,128)(2,1)}, bf16[2,256,1152]{2,1,0:T(8,128)(2,1)S(1)}, u32[]{:S(2)}, u32[]{:S(2)}) collective-permute-start(bf16[2,256,1152]{2,1,0:T(8,128)(2,1)} %pad_maximum_fusion.3), channel_id=1, source_target_pairs={{0,4},{4,0},{8,12},{12,8},{16,20},{20,16},{24,28},{28,24},{1,5},{5... | collective-permute-start | bytes 3538952 | tf_op jit(solution)/shard_map/ppermute | solution.py:369
  60.6 24.8 %collective-permute-start.11 = (bf16[4,72,864]{2,1,0:T(8,128)(2,1)S(1)}, bf16[4,72,864]{2,1,0:T(8,128)(2,1)S(1)}, u32[]{:S(2)}, u32[]{:S(2)}) collective-permute-start(bf16[4,72,864]{2,1,0:T(8,128)(2,1)S(1)} %pad_maximum_fusion.6.refs_0_), channel_id=1, source_target_pairs={{0,16},{4,20},{8,24},{12,28},{16,0},{20,4},{24,8},{28,12},{1,17},{... | collective-permute-start | bytes 1493000 | tf_op jit(solution)/shard_map/ppermute | solution.py:372
  62.2 24.0 %collective-permute-start.12 = (bf16[4,72,864]{2,1,0:T(8,128)(2,1)S(1)}, bf16[4,72,864]{2,1,0:T(8,128)(2,1)}, u32[]{:S(2)}, u32[]{:S(2)}) collective-permute-start(bf16[4,72,864]{2,1,0:T(8,128)(2,1)S(1)} %pad_maximum_fusion.6.refs_0_), channel_id=1, source_target_pairs={{0,24},{4,28},{8,16},{12,20},{16,8},{20,12},{24,0},{28,4},{1,25},{... | collective-permute-start | bytes 1493000 | tf_op jit(solution)/shard_map/ppermute | solution.py:372
  63.6 25.7 %collective-permute-start.16 = (bf16[72,1152]{1,0:T(8,128)(2,1)S(1)}, bf16[72,1152]{1,0:T(8,128)(2,1)}, u32[]{:S(2)}, u32[]{:S(2)}) collective-permute-start(bf16[72,1152]{1,0:T(8,128)(2,1)S(1)} %copy-done.46), channel_id=1, source_target_pairs={{0,0},{1,1},{4,2},{5,3},{2,4},{3,5},{6,6},{7,7},{8,8},{9,9},{12,10... | collective-permute-start | bytes 497672 | tf_op jit(solution)/shard_map/ppermute | solution.py:385
  71.7 17.6 %collective-permute-start.17 = (bf16[72,1152]{1,0:T(8,128)(2,1)S(1)}, bf16[72,1152]{1,0:T(8,128)(2,1)}, u32[]{:S(2)}, u32[]{:S(2)}) collective-permute-start(bf16[72,1152]{1,0:T(8,128)(2,1)S(1)} %copy-done.46), channel_id=1, source_target_pairs={{1,0},{0,1},{5,2},{4,3},{3,4},{2,5},{7,6},{6,7},{9,8},{8,9},{13,10... | collective-permute-start | bytes 497672 | tf_op jit(solution)/shard_map/ppermute | solution.py:385
  90.4 25.9 %collective-permute-start.18 = (bf16[2,72,1152]{2,1,0:T(8,128)(2,1)S(1)}, bf16[2,72,1152]{2,1,0:T(8,128)(2,1)}, u32[]{:S(2)}, u32[]{:S(2)}) collective-permute-start(bf16[2,72,1152]{2,1,0:T(8,128)(2,1)S(1)} %pad_maximum_fusion.12.refs_0_), channel_id=1, source_target_pairs={{0,8},{4,12},{8,0},{12,4},{16,24},{20,28},{24,16},{28,20},{1,9},{5... | collective-permute-start | bytes 995336 | tf_op jit(solution)/shard_map/ppermute | solution.py:372
  91.9 24.5 %collective-permute-start.19 = (bf16[2,72,1152]{2,1,0:T(8,128)(2,1)S(1)}, bf16[2,72,1152]{2,1,0:T(8,128)(2,1)}, u32[]{:S(2)}, u32[]{:S(2)}) collective-permute-start(bf16[2,72,1152]{2,1,0:T(8,128)(2,1)S(1)} %pad_maximum_fusion.12.refs_0_), channel_id=1, source_target_pairs={{0,16},{4,20},{8,24},{12,28},{16,0},{20,4},{24,8},{28,12},{1,17},{... | collective-permute-start | bytes 995336 | tf_op jit(solution)/shard_map/ppermute | solution.py:372
  93.5 23.3 %collective-permute-start.20 = (bf16[2,72,1152]{2,1,0:T(8,128)(2,1)S(1)}, bf16[2,72,1152]{2,1,0:T(8,128)(2,1)}, u32[]{:S(2)}, u32[]{:S(2)}) collective-permute-start(bf16[2,72,1152]{2,1,0:T(8,128)(2,1)S(1)} %pad_maximum_fusion.12.refs_0_), channel_id=1, source_target_pairs={{0,24},{4,28},{8,16},{12,20},{16,8},{20,12},{24,0},{28,4},{1,25},{... | collective-permute-start | bytes 995336 | tf_op jit(solution)/shard_map/ppermute | solution.py:372
  114.7 19.3 %collective-permute-start.36 = (bf16[256,1152]{1,0:T(8,128)(2,1)}, bf16[256,1152]{1,0:T(8,128)(2,1)}, u32[]{:S(2)}, u32[]{:S(2)}) collective-permute-start(bf16[256,1152]{1,0:T(8,128)(2,1)} %fusion.10), channel_id=1, source_target_pairs={{0,8},{4,12},{8,0},{12,4},{16,24},{20,28},{24,16},{28,20},{1,9},{5... | collective-permute-start | bytes 1769480 | tf_op jit(solution)/shard_map/ppermute | solution.py:372
  120.9 35.9 %collective-permute-start.15 = (bf16[2,256,288]{2,1,0:T(8,128)(2,1)S(1)}, bf16[2,256,288]{2,1,0:T(8,128)(2,1)S(1)}, u32[]{:S(2)}, u32[]{:S(2)}) collective-permute-start(bf16[2,256,288]{2,1,0:T(8,128)(2,1)S(1)} %get-tuple-element.200), channel_id=1, source_target_pairs={{1,0},{0,1},{5,2},{4,3},{3,4},{2,5},{7,6},{6,7},{9,8},{8,9},{13,10... | collective-permute-start | bytes 884744 | tf_op jit(solution)/shard_map/ppermute | solution.py:385
  124.7 41.4 %collective-permute-start.29 = (bf16[144,1152]{1,0:T(8,128)(2,1)}, bf16[144,1152]{1,0:T(8,128)(2,1)}, u32[]{:S(2)}, u32[]{:S(2)}) collective-permute-start(bf16[144,1152]{1,0:T(8,128)(2,1)} %take_columns.1), channel_id=1, source_target_pairs={{0,1},{1,2},{2,3},{3,0},{4,5},{5,6},{6,7},{7,4},{8,9},{9,10},{10,1... | collective-permute-start | bytes 995336 | tf_op jit(solution)/shard_map/ppermute | solution.py:366
  125.4 41.2 %collective-permute-start.30 = (bf16[144,1152]{1,0:T(8,128)(2,1)}, bf16[144,1152]{1,0:T(8,128)(2,1)}, u32[]{:S(2)}, u32[]{:S(2)}) collective-permute-start(bf16[144,1152]{1,0:T(8,128)(2,1)} %take_columns.1), channel_id=1, source_target_pairs={{0,2},{1,3},{2,0},{3,1},{4,6},{5,7},{6,4},{7,5},{8,10},{9,11},{10,... | collective-permute-start | bytes 995336 | tf_op jit(solution)/shard_map/ppermute | solution.py:366
  134.1 43.9 %collective-permute-start.35 = (bf16[256,1152]{1,0:T(8,128)(2,1)}, bf16[256,1152]{1,0:T(8,128)(2,1)}, u32[]{:S(2)}, u32[]{:S(2)}) collective-permute-start(bf16[256,1152]{1,0:T(8,128)(2,1)} %fusion.10), channel_id=1, source_target_pairs={{0,4},{4,0},{8,12},{12,8},{16,20},{20,16},{24,28},{28,24},{1,5},{5... | collective-permute-start | bytes 1769480 | tf_op jit(solution)/shard_map/ppermute | solution.py:369
  134.2 44.3 %collective-permute-start.37 = (bf16[256,1152]{1,0:T(8,128)(2,1)}, bf16[256,1152]{1,0:T(8,128)(2,1)}, u32[]{:S(2)}, u32[]{:S(2)}) collective-permute-start(bf16[256,1152]{1,0:T(8,128)(2,1)} %collective-permute-done.36), channel_id=1, source_target_pairs={{0,4},{4,0},{8,12},{12,8},{16,20},{20,16},{24,28},{28,24},{1,5},{5... | collective-permute-start | bytes 1769480 | tf_op jit(solution)/shard_map/ppermute | solution.py:369
  177.9 19.6 %collective-permute-start.34 = (bf16[144,1152]{1,0:T(8,128)(2,1)S(1)}, bf16[144,1152]{1,0:T(8,128)(2,1)}, u32[]{:S(2)}, u32[]{:S(2)}) collective-permute-start(bf16[144,1152]{1,0:T(8,128)(2,1)S(1)} %collective-permute-done.31), channel_id=1, source_target_pairs={{0,16},{4,20},{8,24},{12,28},{16,0},{20,4},{24,8},{28,12},{1,17},{... | collective-permute-start | bytes 995336 | tf_op jit(solution)/shard_map/ppermute | solution.py:372
  178.4 41.2 %collective-permute-start.25 = (bf16[256,1152]{1,0:T(8,128)(2,1)S(1)}, bf16[256,1152]{1,0:T(8,128)(2,1)}, u32[]{:S(2)}, u32[]{:S(2)}) collective-permute-start(bf16[256,1152]{1,0:T(8,128)(2,1)S(1)} %add_convert_fusion.8), channel_id=1, source_target_pairs={{0,4},{4,0},{8,12},{12,8},{16,20},{20,16},{24,28},{28,24},{1,5},{5... | collective-permute-start | bytes 1769480 | tf_op jit(solution)/shard_map/ppermute | solution.py:369
  180.5 40.7 %collective-permute-start.27 = (bf16[256,1152]{1,0:T(8,128)(2,1)}, bf16[256,1152]{1,0:T(8,128)(2,1)}, u32[]{:S(2)}, u32[]{:S(2)}) collective-permute-start(bf16[256,1152]{1,0:T(8,128)(2,1)} %collective-permute-done.26), channel_id=1, source_target_pairs={{0,4},{4,0},{8,12},{12,8},{16,20},{20,16},{24,28},{28,24},{1,5},{5... | collective-permute-start | bytes 1769480 | tf_op jit(solution)/shard_map/ppermute | solution.py:369
  183.3 25.1 %collective-permute-start.39 = (bf16[144,1152]{1,0:T(8,128)(2,1)S(1)}, bf16[144,1152]{1,0:T(8,128)(2,1)}, u32[]{:S(2)}, u32[]{:S(2)}) collective-permute-start(bf16[144,1152]{1,0:T(8,128)(2,1)S(1)} %copy-done.33), channel_id=1, source_target_pairs={{0,1},{1,2},{2,3},{3,0},{4,5},{5,6},{6,7},{7,4},{8,9},{9,10},{10,1... | collective-permute-start | bytes 995336 | tf_op jit(solution)/shard_map/ppermute | solution.py:366
  191.0 21.9 %collective-permute-start.40 = (bf16[144,1152]{1,0:T(8,128)(2,1)S(1)}, bf16[144,1152]{1,0:T(8,128)(2,1)}, u32[]{:S(2)}, u32[]{:S(2)}) collective-permute-start(bf16[144,1152]{1,0:T(8,128)(2,1)S(1)} %copy-done.33), channel_id=1, source_target_pairs={{0,2},{1,3},{2,0},{3,1},{4,6},{5,7},{6,4},{7,5},{8,10},{9,11},{10,... | collective-permute-start | bytes 995336 | tf_op jit(solution)/shard_map/ppermute | solution.py:366
  197.6 20.1 %collective-permute-start.41 = (bf16[144,1152]{1,0:T(8,128)(2,1)S(1)}, bf16[144,1152]{1,0:T(8,128)(2,1)}, u32[]{:S(2)}, u32[]{:S(2)}) collective-permute-start(bf16[144,1152]{1,0:T(8,128)(2,1)S(1)} %copy-done.33), channel_id=1, source_target_pairs={{0,3},{1,0},{2,1},{3,2},{4,7},{5,4},{6,5},{7,6},{8,11},{9,8},{10,9... | collective-permute-start | bytes 995336 | tf_op jit(solution)/shard_map/ppermute | solution.py:366
  208.5 21.8 %collective-permute-start.38 = (bf16[144,1152]{1,0:T(8,128)(2,1)S(1)}, bf16[144,1152]{1,0:T(8,128)(2,1)S(1)}, u32[]{:S(2)}, u32[]{:S(2)}) collective-permute-start(bf16[144,1152]{1,0:T(8,128)(2,1)S(1)} %copy-done.33), channel_id=1, source_target_pairs={{0,16},{4,20},{8,24},{12,28},{16,0},{20,4},{24,8},{28,12},{1,17},{... | collective-permute-start | bytes 995336 | tf_op jit(solution)/shard_map/ppermute | solution.py:372
  219.7 21.6 %collective-permute-start.44 = (bf16[144,1152]{1,0:T(8,128)(2,1)}, bf16[144,1152]{1,0:T(8,128)(2,1)}, u32[]{:S(2)}, u32[]{:S(2)}) collective-permute-start(bf16[144,1152]{1,0:T(8,128)(2,1)} %collective-permute-done.41), channel_id=1, source_target_pairs={{0,16},{4,20},{8,24},{12,28},{16,0},{20,4},{24,8},{28,12},{1,17},{... | collective-permute-start | bytes 995336 | tf_op jit(solution)/shard_map/ppermute | solution.py:372
  260.2 19.6 %collective-permute-start.46 = (bf16[256,1152]{1,0:T(8,128)(2,1)}, bf16[256,1152]{1,0:T(8,128)(2,1)S(1)}, u32[]{:S(2)}, u32[]{:S(2)}) collective-permute-start(bf16[256,1152]{1,0:T(8,128)(2,1)} %get-tuple-element.171), channel_id=1, source_target_pairs={{0,4},{4,0},{8,12},{12,8},{16,20},{20,16},{24,28},{28,24},{1,5},{5... | collective-permute-start | bytes 1769480 | tf_op jit(solution)/shard_map/ppermute | solution.py:369
  277.8 62.1 %collective-permute-start.80 = (bf16[4,144,1152]{2,1,0:T(8,128)(2,1)}, bf16[4,144,1152]{2,1,0:T(8,128)(2,1)}, u32[]{:S(2)}, u32[]{:S(2)}) collective-permute-start(bf16[4,144,1152]{2,1,0:T(8,128)(2,1)} %get-tuple-element.121), channel_id=1, source_target_pairs={{0,16},{4,20},{8,24},{12,28},{16,0},{20,4},{24,8},{28,12},{1,17},{... | collective-permute-start | bytes 3981320 | tf_op jit(solution)/shard_map/ppermute | solution.py:372
  279.3 68.0 %collective-permute-start.84 = (bf16[4,144,1152]{2,1,0:T(8,128)(2,1)}, bf16[4,144,1152]{2,1,0:T(8,128)(2,1)}, u32[]{:S(2)}, u32[]{:S(2)}) collective-permute-start(bf16[4,144,1152]{2,1,0:T(8,128)(2,1)} %get-tuple-element.128), channel_id=1, source_target_pairs={{0,16},{4,20},{8,24},{12,28},{16,0},{20,4},{24,8},{28,12},{1,17},{... | collective-permute-start | bytes 3981320 | tf_op jit(solution)/shard_map/ppermute | solution.py:372
  304.8 47.6 %collective-permute-start.48 = (bf16[256,1152]{1,0:T(8,128)(2,1)}, bf16[256,1152]{1,0:T(8,128)(2,1)}, u32[]{:S(2)}, u32[]{:S(2)}) collective-permute-start(bf16[256,1152]{1,0:T(8,128)(2,1)} %get-tuple-element.169), channel_id=1, source_target_pairs={{0,4},{4,0},{8,12},{12,8},{16,20},{20,16},{24,28},{28,24},{1,5},{5... | collective-permute-start | bytes 1769480 | tf_op jit(solution)/shard_map/ppermute | solution.py:369
  306.3 48.9 %collective-permute-start.50 = (bf16[256,1152]{1,0:T(8,128)(2,1)}, bf16[256,1152]{1,0:T(8,128)(2,1)}, u32[]{:S(2)}, u32[]{:S(2)}) collective-permute-start(bf16[256,1152]{1,0:T(8,128)(2,1)} %add_convert_fusion.6), channel_id=1, source_target_pairs={{0,8},{4,12},{8,0},{12,4},{16,24},{20,28},{24,16},{28,20},{1,9},{5... | collective-permute-start | bytes 1769480 | tf_op jit(solution)/shard_map/ppermute | solution.py:372
  333.6 27.7 %collective-permute-start.54 = (bf16[576,864]{1,0:T(8,128)(2,1)}, bf16[576,864]{1,0:T(8,128)(2,1)}, u32[]{:S(2)}, u32[]{:S(2)}) collective-permute-start(bf16[576,864]{1,0:T(8,128)(2,1)} %get-tuple-element.174), channel_id=1, source_target_pairs={{0,4},{4,0},{8,12},{12,8},{16,20},{20,16},{24,28},{28,24},{1,5},{5... | collective-permute-start | bytes 2985992 | tf_op jit(solution)/shard_map/ppermute | solution.py:369
  343.6 27.8 %collective-permute-start.81 = (bf16[144,1152]{1,0:T(8,128)(2,1)S(1)}, bf16[144,1152]{1,0:T(8,128)(2,1)}, u32[]{:S(2)}, u32[]{:S(2)}) collective-permute-start(bf16[144,1152]{1,0:T(8,128)(2,1)S(1)} %get-tuple-element.177), channel_id=1, source_target_pairs={{0,1},{1,2},{2,3},{3,0},{4,5},{5,6},{6,7},{7,4},{8,9},{9,10},{10,1... | collective-permute-start | bytes 995336 | tf_op jit(solution)/shard_map/ppermute | solution.py:366
  347.3 27.4 %collective-permute-start.82 = (bf16[144,1152]{1,0:T(8,128)(2,1)S(1)}, bf16[144,1152]{1,0:T(8,128)(2,1)}, u32[]{:S(2)}, u32[]{:S(2)}) collective-permute-start(bf16[144,1152]{1,0:T(8,128)(2,1)S(1)} %get-tuple-element.176), channel_id=1, source_target_pairs={{0,2},{1,3},{2,0},{3,1},{4,6},{5,7},{6,4},{7,5},{8,10},{9,11},{10,... | collective-permute-start | bytes 995336 | tf_op jit(solution)/shard_map/ppermute | solution.py:366
  352.4 22.4 %collective-permute-start.83 = (bf16[144,1152]{1,0:T(8,128)(2,1)S(1)}, bf16[144,1152]{1,0:T(8,128)(2,1)}, u32[]{:S(2)}, u32[]{:S(2)}) collective-permute-start(bf16[144,1152]{1,0:T(8,128)(2,1)S(1)} %get-tuple-element.175), channel_id=1, source_target_pairs={{0,3},{1,0},{2,1},{3,2},{4,7},{5,4},{6,5},{7,6},{8,11},{9,8},{10,9... | collective-permute-start | bytes 995336 | tf_op jit(solution)/shard_map/ppermute | solution.py:366
  355.3 22.4 %collective-permute-start.85 = (bf16[144,1152]{1,0:T(8,128)(2,1)S(1)}, bf16[144,1152]{1,0:T(8,128)(2,1)}, u32[]{:S(2)}, u32[]{:S(2)}) collective-permute-start(bf16[144,1152]{1,0:T(8,128)(2,1)S(1)} %get-tuple-element.181), channel_id=1, source_target_pairs={{0,1},{1,2},{2,3},{3,0},{4,5},{5,6},{6,7},{7,4},{8,9},{9,10},{10,1... | collective-permute-start | bytes 995336 | tf_op jit(solution)/shard_map/ppermute | solution.py:366
  361.3 37.3 %collective-permute-start.86 = (bf16[144,1152]{1,0:T(8,128)(2,1)S(1)}, bf16[144,1152]{1,0:T(8,128)(2,1)}, u32[]{:S(2)}, u32[]{:S(2)}) collective-permute-start(bf16[144,1152]{1,0:T(8,128)(2,1)S(1)} %get-tuple-element.180), channel_id=1, source_target_pairs={{0,2},{1,3},{2,0},{3,1},{4,6},{5,7},{6,4},{7,5},{8,10},{9,11},{10,... | collective-permute-start | bytes 995336 | tf_op jit(solution)/shard_map/ppermute | solution.py:366
  371.4 28.3 %collective-permute-start.87 = (bf16[144,1152]{1,0:T(8,128)(2,1)S(1)}, bf16[144,1152]{1,0:T(8,128)(2,1)S(1)}, u32[]{:S(2)}, u32[]{:S(2)}) collective-permute-start(bf16[144,1152]{1,0:T(8,128)(2,1)S(1)} %get-tuple-element.179), channel_id=1, source_target_pairs={{0,3},{1,0},{2,1},{3,2},{4,7},{5,4},{6,5},{7,6},{8,11},{9,8},{10,9... | collective-permute-start | bytes 995336 | tf_op jit(solution)/shard_map/ppermute | solution.py:366
  374.7 39.9 %collective-permute-start.70 = (bf16[576,1152]{1,0:T(8,128)(2,1)}, bf16[576,1152]{1,0:T(8,128)(2,1)}, u32[]{:S(2)}, u32[]{:S(2)}) collective-permute-start(bf16[576,1152]{1,0:T(8,128)(2,1)} %constant_dynamic-slice_fusion.2), channel_id=1, source_target_pairs={{0,4},{4,0},{8,12},{12,8},{16,20},{20,16},{24,28},{28,24},{1,5},{5... | collective-permute-start | bytes 3981320 | tf_op jit(solution)/shard_map/ppermute | solution.py:369
  374.8 45.1 %collective-permute-start.63 = (bf16[2,2,72,864]{3,2,1,0:T(8,128)(2,1)}, bf16[2,2,72,864]{3,2,1,0:T(8,128)(2,1)}, u32[]{:S(2)}, u32[]{:S(2)}) collective-permute-start(bf16[2,2,72,864]{3,2,1,0:T(8,128)(2,1)} %pad_maximum_fusion.10), channel_id=1, source_target_pairs={{0,24},{4,28},{8,16},{12,20},{16,8},{20,12},{24,0},{28,4},{1,25},{... | collective-permute-start | bytes 1493000 | tf_op jit(solution)/shard_map/ppermute | solution.py:372
  377.7 42.2 %collective-permute-start.62 = (bf16[2,2,72,864]{3,2,1,0:T(8,128)(2,1)}, bf16[2,2,72,864]{3,2,1,0:T(8,128)(2,1)}, u32[]{:S(2)}, u32[]{:S(2)}) collective-permute-start(bf16[2,2,72,864]{3,2,1,0:T(8,128)(2,1)} %pad_maximum_fusion.9), channel_id=1, source_target_pairs={{0,16},{4,20},{8,24},{12,28},{16,0},{20,4},{24,8},{28,12},{1,17},{... | collective-permute-start | bytes 1493000 | tf_op jit(solution)/shard_map/ppermute | solution.py:372
  398.6 21.4 %collective-permute-start.61 = (bf16[2,2,72,864]{3,2,1,0:T(8,128)(2,1)}, bf16[2,2,72,864]{3,2,1,0:T(8,128)(2,1)}, u32[]{:S(2)}, u32[]{:S(2)}) collective-permute-start(bf16[2,2,72,864]{3,2,1,0:T(8,128)(2,1)} %pad_maximum_fusion.8), channel_id=1, source_target_pairs={{0,8},{4,12},{8,0},{12,4},{16,24},{20,28},{24,16},{28,20},{1,9},{5... | collective-permute-start | bytes 1493000 | tf_op jit(solution)/shard_map/ppermute | solution.py:372
  400.4 22.8 %collective-permute-start.58 = (f32[1,18432]{1,0:T(1,128)}, f32[1,18432]{1,0:T(1,128)S(1)}, u32[]{:S(2)}, u32[]{:S(2)}) collective-permute-start(f32[1,18432]{1,0:T(1,128)} %constant_dynamic-update-slice_fusion.2), channel_id=1, source_target_pairs={{0,1},{1,2},{2,3},{3,0},{4,5},{5,6},{6,7},{7,4},{8,9},{9,10},{10,1... | collective-permute-start | bytes 221192 | tf_op jit(solution)/shard_map/ppermute | solution.py:366
  419.9 55.9 %collective-permute-start.55 = (bf16[512,1152]{1,0:T(8,128)(2,1)}, bf16[512,1152]{1,0:T(8,128)(2,1)}, u32[]{:S(2)}, u32[]{:S(2)}) collective-permute-start(bf16[512,1152]{1,0:T(8,128)(2,1)} %slice.225), channel_id=1, source_target_pairs={{0,4},{4,0},{8,12},{12,8},{16,20},{20,16},{24,28},{28,24},{1,5},{5... | collective-permute-start | bytes 3538952 | tf_op jit(solution)/shard_map/ppermute | solution.py:369
  425.3 17.9 %collective-permute-start.77 = (bf16[2,72,864]{2,1,0:T(8,128)(2,1)S(1)}, bf16[2,72,864]{2,1,0:T(8,128)(2,1)S(1)}, u32[]{:S(2)}, u32[]{:S(2)}) collective-permute-start(bf16[2,72,864]{2,1,0:T(8,128)(2,1)S(1)} %get-tuple-element.210), channel_id=1, source_target_pairs={{0,0},{1,1},{2,4},{3,5},{4,2},{5,3},{6,6},{7,7},{8,8},{9,9},{10,12... | collective-permute-start | bytes 746504 | tf_op jit(solution)/shard_map/ppermute | solution.py:388
  453.7 76.0 %all-gather.7.cloned.1.call-start = ((), (), s32[]{:S(2)}) async-start(), calls=%async_computation.1 | async-start | bytes 5971968 | tf_op jit(solution)/shard_map/all_gather | solution.py:599
  (101 other events, 1005.9 us)
Sparse Core Ops, SparseCore 0:
  453.8 32.6 all-gather.4
  488.4 41.2 all-gather.6
